TPU v7x, 32 devices: a whole 2x2x4 slice. The times are simulated.
32 devices in a mesh: dp: 8 (over z, y), fsdp: 4 (over x, core).
Axes of the slice: x: 2, y: 2, z: 4, core: 2. Of those that a mesh axis runs over, the one named last changes fastest.
Arguments:
- tokens: bfloat16 [64, 1024, 768], P(('dp', 'fsdp')), may hold values from -6 to 6
- seg_ids: int32 [64, 1024], P(('dp', 'fsdp')), may hold values from 0 to 17, as said below
- pad_mask: int32 [64, 1024], P(('dp', 'fsdp')), may hold values from 0 to 1, as said below
- w_query: bfloat16 [768, 768], P(('dp', 'fsdp')), may hold values from -0.625 to 0.625
- w_key: bfloat16 [768, 768], P(('dp', 'fsdp')), may hold values from -0.625 to 0.625
- w_value: bfloat16 [768, 768], P(('dp', 'fsdp')), may hold values from -0.21875 to 0.21875
- w_out: bfloat16 [768, 768], P(('dp', 'fsdp')), may hold values from -0.625 to 0.625
- w_in: bfloat16 [768, 3072], P(('dp', 'fsdp')), may hold values from -0.21875 to 0.21875
- w_back: bfloat16 [3072, 768], P(('dp', 'fsdp')), may hold values from -0.109375 to 0.109375
- b_query: bfloat16 [768], P(('dp', 'fsdp')), may hold values from -6 to 6
- b_value: bfloat16 [768], P(('dp', 'fsdp')), may hold values from -3 to 3
- b_out: bfloat16 [768], P(('dp', 'fsdp')), may hold values from -1.75 to 1.75
- gain_attn: bfloat16 [768], P(('dp', 'fsdp')), may hold values from 0.5 to 1.5
- shift_attn: bfloat16 [768], P(('dp', 'fsdp')), may hold values from -1.75 to 1.75
- b_in: bfloat16 [3072], P(('dp', 'fsdp')), may hold values from -3 to 3
- b_back: bfloat16 [768], P(('dp', 'fsdp')), may hold values from -1.75 to 1.75
- gain_ffn: bfloat16 [768], P(('dp', 'fsdp')), may hold values from 0.5 to 1.5
- shift_ffn: bfloat16 [768], P(('dp', 'fsdp')), may hold values from -1.75 to 1.75
- conv_weight: bfloat16 [12, 33], replicated, may hold values from -0.375 to 0.375
- cotangent: bfloat16 [64, 1024, 768], P(('dp', 'fsdp')), may hold values from -6 to 6
Outputs:
- output: bfloat16 [64, 1024, 768], P(('dp', 'fsdp'))
- grad_tokens: bfloat16 [64, 1024, 768], P(('dp', 'fsdp'))
- grad_w_query: float32 [768, 768], P(('dp', 'fsdp'))
- grad_w_key: float32 [768, 768], P(('dp', 'fsdp'))
- grad_w_value: float32 [768, 768], P(('dp', 'fsdp'))
- grad_w_out: float32 [768, 768], P(('dp', 'fsdp'))
- grad_w_in: float32 [768, 3072], P(('dp', 'fsdp'))
- grad_w_back: float32 [3072, 768], P(('dp', 'fsdp'))
- grad_b_query: float32 [768], P(('dp', 'fsdp'))
- grad_b_value: float32 [768], P(('dp', 'fsdp'))
- grad_b_out: float32 [768], P(('dp', 'fsdp'))
- grad_gain_attn: float32 [768], P(('dp', 'fsdp'))
- grad_shift_attn: float32 [768], P(('dp', 'fsdp'))
- grad_b_in: float32 [3072], P(('dp', 'fsdp'))
- grad_b_back: float32 [768], P(('dp', 'fsdp'))
- grad_gain_ffn: float32 [768], P(('dp', 'fsdp'))
- grad_shift_ffn: float32 [768], P(('dp', 'fsdp'))
- grad_conv: float32 [12, 33], replicated
Inputs may be any that keep to these rules, and one draw needn't show every extreme that they name: `seg_ids`: within a sequence the live tokens form whole documents of 60 to 800 tokens numbered 0, 1, 2 and so on in order; every padding token carries the number 1024 // 60. `pad_mask`: 1 on each sequence's tokens up to the end of its last whole document, 0 after; the last token of every sequence is padding.
All inputs are finite; a program needn't handle non-finite values.
Results may differ from a plain program's by a relative error of at most 0.025.
The roundings to bfloat16 on the way count: a program that leaves them out, or rounds other values in their place, can miss the bound.
Values may be sent and summed in bfloat16 or wider, within the bound.
A program may use at most 384 MiB of HBM per device.

v0:
```python
from functools import partial

import jax
import jax.numpy as jnp
from jax import lax
from jax.sharding import PartitionSpec as P

LAND = 64
PINV_STEPS = 6
MICRO = 2


precise = lax.Precision.HIGHEST
neg_fill = -1e30
norm_eps = 1e-05


def layouts(segments, padding, land_total):
    length = segments.shape[1]
    stride = length // land_total
    lead_seg = segments[:, ::stride]
    lead_live = padding[:, ::stride] == 1
    token_block = jnp.arange(length, dtype=jnp.int32) // stride
    land_index = jnp.arange(land_total, dtype=jnp.int32)
    same_doc = segments[:, None, :] == lead_seg[:, :, None]
    cross_mask = same_doc & (padding[:, None, :] == 1) & lead_live[:, :, None]
    member = cross_mask & (token_block[None, None, :] == land_index[None, :, None])
    among_mask = (
        (lead_seg[:, :, None] == lead_seg[:, None, :])
        & lead_live[:, :, None]
        & lead_live[:, None, :]
    )
    land_count = jnp.maximum(jnp.sum(member.astype(jnp.float32), axis=2), 1.0)
    return (member, land_count, cross_mask, among_mask, lead_live.astype(jnp.float32))


def masked_softmax(scores, mask, axis):
    held_scores = jnp.where(mask, scores, neg_fill)
    row_top = jnp.max(held_scores, axis=axis, keepdims=True)
    exp_terms = jnp.exp(held_scores - row_top)
    return exp_terms / jnp.sum(exp_terms, axis=axis, keepdims=True)


def newton_pinv(matrix, step_count):
    order_size = matrix.shape[-1]
    identity = jnp.eye(order_size, dtype=matrix.dtype)
    frob_norm = jnp.sum(matrix * matrix, axis=(-2, -1), keepdims=True) + 1e-06
    inverse = jnp.swapaxes(matrix, -1, -2) / frob_norm
    for iteration in range(step_count):
        product = jnp.einsum("...ij,...jk->...ik", matrix, inverse, precision=precise)
        bracket = 7.0 * identity - product
        bracket = 15.0 * identity - jnp.einsum(
            "...ij,...jk->...ik", product, bracket, precision=precise
        )
        bracket = 13.0 * identity - jnp.einsum(
            "...ij,...jk->...ik", product, bracket, precision=precise
        )
        inverse = 0.25 * jnp.einsum("...ij,...jk->...ik", inverse, bracket, precision=precise)
    return inverse


def convolve(value_rows, kernel, segments, padding, head_dim):
    seq_count, length, model_width = value_rows.shape
    head_count, tap_count = kernel.shape
    half_span = tap_count // 2
    block = min(128, length)
    block_count = length // block
    window = block + 2 * half_span
    value_pad = jnp.pad(value_rows, ((0, 0), (half_span, half_span), (0, 0)))
    seg_pad = jnp.pad(segments, ((0, 0), (half_span, half_span)), constant_values=-1)
    live_pad = jnp.pad(padding, ((0, 0), (half_span, half_span)))
    value_win = jnp.stack(
        [value_pad[:, blk * block : blk * block + window] for blk in range(block_count)], axis=1
    )
    value_win = value_win.reshape(seq_count, block_count, window, head_count, head_dim)
    seg_win = jnp.stack(
        [seg_pad[:, blk * block : blk * block + window] for blk in range(block_count)], axis=1
    )
    live_win = jnp.stack(
        [live_pad[:, blk * block : blk * block + window] for blk in range(block_count)], axis=1
    )
    own_seg = segments.reshape(seq_count, block_count, block)
    relative = (
        jnp.arange(window, dtype=jnp.int32)[None, :] - jnp.arange(block, dtype=jnp.int32)[:, None]
    )
    tap_table = (
        relative[:, :, None] == jnp.arange(tap_count, dtype=jnp.int32)[None, None, :]
    ).astype(jnp.float32)
    tap_band = jnp.einsum("irk,hk->hir", tap_table, kernel, precision=precise)
    kept = (
        (seg_win[:, :, None, :] == own_seg[:, :, :, None]) & (live_win[:, :, None, :] == 1)
    ).astype(jnp.float32)
    band = kept[:, :, None, :, :] * tap_band[None, None]
    result = jnp.einsum("bnhir,bnrhe->bnihe", band, value_win, precision=precise)
    return result.reshape(seq_count, length, model_width)


def layer_norm(resid, gain, shift):
    row_mean = jnp.mean(resid, axis=-1, keepdims=True)
    centered = resid - row_mean
    variance = jnp.mean(centered * centered, axis=-1, keepdims=True)
    return centered * lax.rsqrt(variance + norm_eps) * gain + shift


def gather_weights(w_query, w_key, w_value, w_out, w_in, w_back, b_in, vectors):
    return (
        lax.all_gather(w_query, ("dp", "fsdp"), axis=0, tiled=True),
        lax.all_gather(w_key, ("dp", "fsdp"), axis=0, tiled=True),
        lax.all_gather(w_value, ("dp", "fsdp"), axis=0, tiled=True),
        lax.all_gather(w_out, ("dp", "fsdp"), axis=0, tiled=True),
        lax.all_gather(w_in, ("dp", "fsdp"), axis=0, tiled=True),
        lax.all_gather(w_back, ("dp", "fsdp"), axis=0, tiled=True),
        lax.all_gather(b_in, ("dp", "fsdp"), axis=0, tiled=True),
        lax.all_gather(vectors, ("dp", "fsdp"), axis=0, tiled=True),
    )


def forward_pass(weights, kernel, tokens_mb, segments, padding):
    w_query, w_key, w_value, w_out, w_in, w_back, b_in, vectors = weights
    biases = vectors.astype(jnp.float32)
    seq_count, length, model_width = tokens_mb.shape
    head_count = kernel.shape[0]
    head_dim = model_width // head_count
    score_scale = head_dim ** (-0.5)
    rows_total = seq_count * length
    heads_shape = (seq_count, length, head_count, head_dim)
    member, land_count, cross_mask, among_mask, land_live = layouts(segments, padding, LAND)
    member_low = member.astype(jnp.bfloat16)
    flat_rows = tokens_mb.reshape(rows_total, model_width)
    query_low = (
        (jnp.dot(flat_rows, w_query, preferred_element_type=jnp.float32) + biases[:, 0])
        .astype(jnp.bfloat16)
        .reshape(heads_shape)
    )
    key_low = (
        jnp.dot(flat_rows, w_key, preferred_element_type=jnp.float32)
        .astype(jnp.bfloat16)
        .reshape(heads_shape)
    )
    value_low = (
        (jnp.dot(flat_rows, w_value, preferred_element_type=jnp.float32) + biases[:, 1])
        .astype(jnp.bfloat16)
        .reshape(heads_shape)
    )
    land_query = (
        jnp.einsum("bjt,bthe->bjhe", member_low, query_low, preferred_element_type=jnp.float32)
        / land_count[:, :, None, None]
    ).astype(jnp.bfloat16)
    land_key = (
        jnp.einsum("bjt,bthe->bjhe", member_low, key_low, preferred_element_type=jnp.float32)
        / land_count[:, :, None, None]
    ).astype(jnp.bfloat16)
    score_f = (
        jnp.einsum("bjhe,bthe->bhjt", land_key, query_low, preferred_element_type=jnp.float32)
        * score_scale
    )
    kern_f = masked_softmax(score_f, cross_mask[:, None], -2).astype(jnp.bfloat16)
    score_b = (
        jnp.einsum("bjhe,bthe->bhjt", land_query, key_low, preferred_element_type=jnp.float32)
        * score_scale
    )
    kern_b = (
        masked_softmax(score_b, cross_mask[:, None], -1) * land_live[:, None, :, None]
    ).astype(jnp.bfloat16)
    score_a = (
        jnp.einsum("bihe,bjhe->bhij", land_query, land_key, preferred_element_type=jnp.float32)
        * score_scale
    )
    kern_a = masked_softmax(score_a, among_mask[:, None], -1) * land_live[:, None, :, None]
    inverse = newton_pinv(kern_a, PINV_STEPS)
    summary = jnp.einsum("bhjt,bthe->bhje", kern_b, value_low, preferred_element_type=jnp.float32)
    mixed_low = jnp.einsum("bhij,bhje->bhie", inverse, summary, precision=precise).astype(
        jnp.bfloat16
    )
    approx = jnp.einsum(
        "bhjt,bhje->bthe", kern_f, mixed_low, preferred_element_type=jnp.float32
    ).reshape(seq_count, length, model_width)
    value_rows = value_low.reshape(seq_count, length, model_width).astype(jnp.float32)
    local_conv = convolve(value_rows, kernel, segments, padding, head_dim)
    pad_rows = padding.astype(jnp.float32)[:, :, None]
    attended = (
        ((approx + local_conv) * pad_rows).reshape(rows_total, model_width).astype(jnp.bfloat16)
    )
    branch = jnp.dot(attended, w_out, preferred_element_type=jnp.float32) + biases[:, 2]
    first_resid = flat_rows.astype(jnp.float32) + branch
    hidden = layer_norm(first_resid, biases[:, 3], biases[:, 4])
    hidden_low = hidden.astype(jnp.bfloat16)
    inner_act = jnp.dot(hidden_low, w_in, preferred_element_type=jnp.float32) + b_in.astype(
        jnp.float32
    )
    active = jax.nn.gelu(inner_act, approximate=False).astype(jnp.bfloat16)
    feed_out = jnp.dot(active, w_back, preferred_element_type=jnp.float32) + biases[:, 5]
    second_resid = hidden + feed_out
    result = layer_norm(second_resid, biases[:, 6], biases[:, 7])
    saved = (
        member,
        land_count,
        cross_mask,
        among_mask,
        land_live,
        query_low,
        key_low,
        value_low,
        land_query,
        land_key,
        score_f,
        score_b,
        score_a,
        kern_f,
        kern_b,
        inverse,
        summary,
        mixed_low,
        value_rows,
        attended,
        first_resid,
        hidden_low,
        inner_act,
        active,
        second_resid,
    )
    return (result.reshape(seq_count, length, model_width).astype(jnp.bfloat16), saved)


def backward_pass(weights, kernel, tokens_mb, segments, padding, saved, cotangent_mb):
    w_query, w_key, w_value, w_out, w_in, w_back, b_in, vectors = weights
    biases = vectors.astype(jnp.float32)
    (
        member,
        land_count,
        cross_mask,
        among_mask,
        land_live,
        query_low,
        key_low,
        value_low,
        land_query,
        land_key,
        score_f,
        score_b,
        score_a,
        kern_f,
        kern_b,
        inverse,
        summary,
        mixed_low,
        value_rows,
        attended,
        first_resid,
        hidden_low,
        inner_act,
        active,
        second_resid,
    ) = saved
    seq_count, length, model_width = tokens_mb.shape
    head_count = kernel.shape[0]
    head_dim = model_width // head_count
    score_scale = head_dim ** (-0.5)
    rows_total = seq_count * length
    heads_shape = (seq_count, length, head_count, head_dim)
    flat_rows = tokens_mb.reshape(rows_total, model_width)
    grad_out = cotangent_mb.reshape(rows_total, model_width).astype(jnp.float32)
    unused_second, norm_second = jax.vjp(layer_norm, second_resid, biases[:, 6], biases[:, 7])
    grad_second, grad_gain_ffn, grad_shift_ffn = norm_second(grad_out)
    grad_feed = grad_second.astype(jnp.bfloat16)
    grad_w_back = jnp.einsum("tf,td->fd", active, grad_feed, preferred_element_type=jnp.float32)
    grad_b_back = jnp.sum(grad_feed.astype(jnp.float32), axis=0)
    grad_active = jnp.einsum("td,fd->tf", grad_feed, w_back, preferred_element_type=jnp.float32)
    unused_gelu, gelu_back = jax.vjp(partial(jax.nn.gelu, approximate=False), inner_act)
    grad_inner = gelu_back(grad_active)[0].astype(jnp.bfloat16)
    grad_w_in = jnp.einsum("td,tf->df", hidden_low, grad_inner, preferred_element_type=jnp.float32)
    grad_b_in = jnp.sum(grad_inner.astype(jnp.float32), axis=0)
    grad_hidden = grad_second + jnp.einsum(
        "tf,df->td", grad_inner, w_in, preferred_element_type=jnp.float32
    )
    unused_first, norm_first = jax.vjp(layer_norm, first_resid, biases[:, 3], biases[:, 4])
    grad_first, grad_gain_attn, grad_shift_attn = norm_first(grad_hidden)
    grad_branch = grad_first.astype(jnp.bfloat16)
    grad_w_out = jnp.einsum("tc,td->cd", attended, grad_branch, preferred_element_type=jnp.float32)
    grad_b_out = jnp.sum(grad_branch.astype(jnp.float32), axis=0)
    grad_attended = jnp.einsum(
        "td,cd->tc", grad_branch, w_out, preferred_element_type=jnp.float32
    ).astype(jnp.bfloat16)
    grad_approx = (
        grad_attended.reshape(seq_count, length, model_width)
        * padding.astype(jnp.bfloat16)[:, :, None]
    )
    unused_conv, conv_back = jax.vjp(
        lambda rows_in, taps_in: convolve(rows_in, taps_in, segments, padding, head_dim),
        value_rows,
        kernel,
    )
    grad_conv_rows, grad_kernel = conv_back(grad_approx.astype(jnp.float32))
    grad_heads = grad_approx.reshape(heads_shape)
    grad_kern_f = jnp.einsum(
        "bthe,bhje->bhjt", grad_heads, mixed_low, preferred_element_type=jnp.float32
    )
    grad_mixed = jnp.einsum(
        "bhjt,bthe->bhje", kern_f, grad_heads, preferred_element_type=jnp.float32
    )
    grad_inverse = jnp.einsum("bhie,bhje->bhij", grad_mixed, summary, precision=precise)
    grad_summary = jnp.einsum("bhij,bhie->bhje", inverse, grad_mixed, precision=precise).astype(
        jnp.bfloat16
    )
    grad_kern_b = jnp.einsum(
        "bhje,bthe->bhjt", grad_summary, value_low, preferred_element_type=jnp.float32
    )
    grad_value = (
        jnp.einsum(
            "bhjt,bhje->bthe", kern_b, grad_summary, preferred_element_type=jnp.float32
        ).reshape(seq_count, length, model_width)
        + grad_conv_rows
    )
    unused_a, back_a = jax.vjp(
        lambda scores: newton_pinv(
            masked_softmax(scores, among_mask[:, None], -1) * land_live[:, None, :, None],
            PINV_STEPS,
        ),
        score_a,
    )
    grad_score_a = back_a(grad_inverse)[0].astype(jnp.bfloat16)
    unused_b, back_b = jax.vjp(
        lambda scores: masked_softmax(scores, cross_mask[:, None], -1)
        * land_live[:, None, :, None],
        score_b,
    )
    grad_score_b = back_b(grad_kern_b)[0].astype(jnp.bfloat16)
    unused_f, back_f = jax.vjp(
        lambda scores: masked_softmax(scores, cross_mask[:, None], -2), score_f
    )
    grad_score_f = back_f(grad_kern_f)[0].astype(jnp.bfloat16)
    grad_query = (
        jnp.einsum("bhjt,bjhe->bthe", grad_score_f, land_key, preferred_element_type=jnp.float32)
        * score_scale
    )
    grad_land_key = (
        jnp.einsum("bhjt,bthe->bjhe", grad_score_f, query_low, preferred_element_type=jnp.float32)
        + jnp.einsum(
            "bhij,bihe->bjhe", grad_score_a, land_query, preferred_element_type=jnp.float32
        )
    ) * score_scale
    grad_key = (
        jnp.einsum("bhjt,bjhe->bthe", grad_score_b, land_query, preferred_element_type=jnp.float32)
        * score_scale
    )
    grad_land_query = (
        jnp.einsum("bhjt,bthe->bjhe", grad_score_b, key_low, preferred_element_type=jnp.float32)
        + jnp.einsum("bhij,bjhe->bihe", grad_score_a, land_key, preferred_element_type=jnp.float32)
    ) * score_scale
    member_full = member.astype(jnp.float32)
    grad_query = grad_query + jnp.einsum(
        "bjt,bjhe->bthe",
        member_full,
        grad_land_query / land_count[:, :, None, None],
        precision=precise,
    )
    grad_key = grad_key + jnp.einsum(
        "bjt,bjhe->bthe",
        member_full,
        grad_land_key / land_count[:, :, None, None],
        precision=precise,
    )
    grad_query_low = grad_query.reshape(rows_total, model_width).astype(jnp.bfloat16)
    grad_key_low = grad_key.reshape(rows_total, model_width).astype(jnp.bfloat16)
    grad_value_low = grad_value.reshape(rows_total, model_width).astype(jnp.bfloat16)
    grad_w_query = jnp.einsum(
        "tc,td->cd", flat_rows, grad_query_low, preferred_element_type=jnp.float32
    )
    grad_w_key = jnp.einsum(
        "tc,td->cd", flat_rows, grad_key_low, preferred_element_type=jnp.float32
    )
    grad_w_value = jnp.einsum(
        "tc,td->cd", flat_rows, grad_value_low, preferred_element_type=jnp.float32
    )
    grad_b_query = jnp.sum(grad_query_low.astype(jnp.float32), axis=0)
    grad_b_value = jnp.sum(grad_value_low.astype(jnp.float32), axis=0)
    grad_rows = grad_first + jnp.einsum(
        "td,cd->tc", grad_query_low, w_query, preferred_element_type=jnp.float32
    )
    grad_rows = grad_rows + jnp.einsum(
        "td,cd->tc", grad_key_low, w_key, preferred_element_type=jnp.float32
    )
    grad_rows = grad_rows + jnp.einsum(
        "td,cd->tc", grad_value_low, w_value, preferred_element_type=jnp.float32
    )
    grad_vectors = jnp.stack(
        [
            grad_b_query,
            grad_b_value,
            grad_b_out,
            grad_gain_attn,
            grad_shift_attn,
            grad_b_back,
            grad_gain_ffn,
            grad_shift_ffn,
        ],
        axis=1,
    )
    grads = (
        grad_w_query,
        grad_w_key,
        grad_w_value,
        grad_w_out,
        grad_w_in,
        grad_w_back,
        grad_b_in,
        grad_vectors,
        grad_kernel,
    )
    return (grad_rows.reshape(seq_count, length, model_width).astype(jnp.bfloat16), grads)


def per_device(
    tokens,
    seg_ids,
    pad_mask,
    w_query,
    w_key,
    w_value,
    w_out,
    w_in,
    w_back,
    b_query,
    b_value,
    b_out,
    gain_attn,
    shift_attn,
    b_in,
    b_back,
    gain_ffn,
    shift_ffn,
    conv_weight,
    cotangent,
):
    vectors = jnp.stack(
        [b_query, b_value, b_out, gain_attn, shift_attn, b_back, gain_ffn, shift_ffn], axis=1
    )
    kernel = conv_weight.astype(jnp.float32)
    per_micro = tokens.shape[0] // MICRO
    totals = None
    result_parts = []
    grad_parts = []
    for micro in range(MICRO):
        begin = micro * per_micro
        tokens_mb = tokens[begin : begin + per_micro]
        segments = seg_ids[begin : begin + per_micro]
        padding = pad_mask[begin : begin + per_micro]
        weights = gather_weights(w_query, w_key, w_value, w_out, w_in, w_back, b_in, vectors)
        result, saved = forward_pass(weights, kernel, tokens_mb, segments, padding)
        weights = gather_weights(w_query, w_key, w_value, w_out, w_in, w_back, b_in, vectors)
        grad_rows, grads = backward_pass(
            weights,
            kernel,
            tokens_mb,
            segments,
            padding,
            saved,
            cotangent[begin : begin + per_micro],
        )
        totals = grads if totals is None else jax.tree.map(jnp.add, totals, grads)
        result_parts.append(result)
        grad_parts.append(grad_rows)
    shares = (
        lax.psum_scatter(totals[0], ("dp", "fsdp"), scatter_dimension=0, tiled=True),
        lax.psum_scatter(totals[1], ("dp", "fsdp"), scatter_dimension=0, tiled=True),
        lax.psum_scatter(totals[2], ("dp", "fsdp"), scatter_dimension=0, tiled=True),
        lax.psum_scatter(totals[3], ("dp", "fsdp"), scatter_dimension=0, tiled=True),
        lax.psum_scatter(totals[4], ("dp", "fsdp"), scatter_dimension=0, tiled=True),
        lax.psum_scatter(totals[5], ("dp", "fsdp"), scatter_dimension=0, tiled=True),
        lax.psum_scatter(totals[6], ("dp", "fsdp"), scatter_dimension=0, tiled=True),
        lax.psum_scatter(totals[7], ("dp", "fsdp"), scatter_dimension=0, tiled=True),
    )
    grad_kernel = lax.psum(totals[8], ("dp", "fsdp"))
    output = jnp.concatenate(result_parts, axis=0)
    grad_tokens = jnp.concatenate(grad_parts, axis=0)
    vector_share = shares[7]
    return (
        output,
        grad_tokens,
        shares[0],
        shares[1],
        shares[2],
        shares[3],
        shares[4],
        shares[5],
        vector_share[:, 0],
        vector_share[:, 1],
        vector_share[:, 2],
        vector_share[:, 3],
        vector_share[:, 4],
        shares[6],
        vector_share[:, 5],
        vector_share[:, 6],
        vector_share[:, 7],
        grad_kernel,
    )


def solution(mesh):
    in_specs = (
        P(("dp", "fsdp"), None, None),
        P(("dp", "fsdp"), None),
        P(("dp", "fsdp"), None),
        P(("dp", "fsdp"), None),
        P(("dp", "fsdp"), None),
        P(("dp", "fsdp"), None),
        P(("dp", "fsdp"), None),
        P(("dp", "fsdp"), None),
        P(("dp", "fsdp"), None),
        P(("dp", "fsdp")),
        P(("dp", "fsdp")),
        P(("dp", "fsdp")),
        P(("dp", "fsdp")),
        P(("dp", "fsdp")),
        P(("dp", "fsdp")),
        P(("dp", "fsdp")),
        P(("dp", "fsdp")),
        P(("dp", "fsdp")),
        P(),
        P(("dp", "fsdp"), None, None),
    )
    out_specs = (
        P(("dp", "fsdp"), None, None),
        P(("dp", "fsdp"), None, None),
        P(("dp", "fsdp"), None),
        P(("dp", "fsdp"), None),
        P(("dp", "fsdp"), None),
        P(("dp", "fsdp"), None),
        P(("dp", "fsdp"), None),
        P(("dp", "fsdp"), None),
        P(("dp", "fsdp")),
        P(("dp", "fsdp")),
        P(("dp", "fsdp")),
        P(("dp", "fsdp")),
        P(("dp", "fsdp")),
        P(("dp", "fsdp")),
        P(("dp", "fsdp")),
        P(("dp", "fsdp")),
        P(("dp", "fsdp")),
        P(),
    )
    return jax.shard_map(
        per_device, mesh=mesh, in_specs=in_specs, out_specs=out_specs, check_vma=False
    )
```

profile of v0, /device:TPU:0, one launch (start us, length us, event | category | flops | bytes accessed | tf_op | source)
XLA Modules:
  0.0 1371.2 jit_solution(4812511429577384296)
XLA Ops:
  22.4 43.4 %all-gather = bf16[32,24,8]{1,2,0:T(8,128)(2,1)S(1)} all-gather(bf16[1,24,8]{1,2,0:T(8,128)(2,1)S(1)} %bitcast.1537), channel_id=1, replica_groups=mesh['dp'=8,'fsdp'=4] {'dp','fsdp'}, dimensions={0}, use_global_device_ids=true | all-gather | bytes 12672 | tf_op jit(solution)/shard_map/all_gather | solution.py:114
  75.2 37.7 %all-reduce.22 = bf16[3072]{0:T(1024)(128)(2,1)S(1)} all-reduce(bf16[3072]{0:T(1024)(128)(2,1)S(1)} %dynamic-update-slice), channel_id=1, replica_groups=mesh['dp'=8,'fsdp'=4] {'dp','fsdp'}, use_global_device_ids=true, to_apply=%add.22 | all-reduce | flops 3072 | bytes 12288
  138.0 6.6 convert_reduce_fusion.12
  162.6 6.4 convert_reduce_fusion.14
  192.2 5.3 bitcast_convert_fusion.1
  232.7 10.0 fusion.89
  315.4 10.0 fusion.94
  338.5 8.0 fusion.440
  351.0 68.6 %multiply_convert_fusion.1 = (bf16[1024,3072]{1,0:T(8,128)(2,1)}, f32[1024,3072]{1,0:T(8,128)}, bf16[1024,3072]{1,0:T(8,128)(2,1)}, f32[1024,3072]{1,0:T(8,128)}, f32[1024,3072]{1,0:T(8,128)}) fusion(f32[3072]{0:T(1024)S(1)} %convert_element_type.388, f32[1024,3072]{1,0:T(8,128)S(1)} %fusion.440, bf16[768,3072]{1,0:T(8,128)(2,1)S(1)} %copy-done.114, ...), kind=kOutput, calls=%fused_computation.21 | convolution fusion | flops 5247074304 | bytes 69218304 | tf_op jit(solution)/shard_map/dot_general | solution.py:188
  419.7 9.1 fusion.479
  428.9 8.7 fusion.480
  445.5 5.9 convert_reduce_fusion.4
  451.5 19.0 %convert_reduce_fusion = (f32[3072]{0:T(1024)}, bf16[1024,3072]{1,0:T(8,128)(2,1)}) fusion(f32[1024,3072]{1,0:T(8,128)} %get-tuple-element.248, bf16[1024,768]{0,1:T(8,128)(2,1)} %get-tuple-element.154, bf16[3072,768]{1,0:T(8,128)(2,1)} %all-gather.18.cloned.1.call-done, f32[1024,3072]{1,0:T(8,128)} %copy-done.83, f32[3072]{0:T(1024)S(1)} %convert_element_type.388), kind=kOutput, calls=%fused_computation.4 | convolution fusion | flops 4885312512 | bytes 37773312 | tf_op jit(solution)/shard_map/td,fd->tf/dot_general | solution.py:268
  470.5 10.7 add_add_fusion.8
  481.2 19.2 %convert_reduce_fusion.1 = (f32[3072]{0:T(1024)}, bf16[1024,3072]{1,0:T(8,128)(2,1)}) fusion(f32[1024,3072]{1,0:T(8,128)} %get-tuple-element.190, bf16[1024,768]{0,1:T(8,128)(2,1)} %get-tuple-element.251, bf16[3072,768]{1,0:T(8,128)(2,1)} %all-gather.18.cloned.1.call-done, f32[1024,3072]{1,0:T(8,128)} %get-tuple-element.329, f32[3072]{0:T(1024)S(1)} %convert_element_type.388), kind=kOutput, calls=%fused_computation.5 | convolution fusion | flops 4885312512 | bytes 37773312 | tf_op jit(solution)/shard_map/td,fd->tf/dot_general | solution.py:268
  500.4 13.4 multiply_reduce_fusion.3
  633.4 8.0 fusion.12
  654.8 8.0 fusion.16
  668.6 6.1 fusion.62
  693.3 8.9 fusion.458
  706.8 7.4 fusion.464
  759.1 8.0 fusion.508
  767.0 10.9 convolution_add_fusion
  779.9 7.7 fusion.442
  787.6 10.9 convolution_add_fusion.1
  828.0 11.2 multiply_reduce_fusion.1
  841.2 8.3 multiply_reduce_fusion
  851.6 42.2 %all-reduce.25 = (f32[768,8]{0,1:T(8,128)S(1)}, f32[3072]{0:T(1024)S(1)}, f32[12,33]{1,0:T(8,128)}) all-reduce(f32[768,8]{0,1:T(8,128)S(1)} %add.433, f32[3072]{0:T(1024)S(1)} %add.434, f32[12,33]{1,0:T(8,128)S(1)} %fusion.287), channel_id=8, replica_groups=mesh['dp'=8,'fsdp'=4] {'dp','fsdp'}, use_global_device_ids=true, to_apply=%region_74.75.clone | all-reduce | flops 9612 | bytes 76896
  895.0 81.7 %reduce-scatter.22.cloned.1.call-done = f32[24,768]{1,0:T(8,128)} async-done(((f32[768,768]{1,0:T(8,128)}), f32[24,768]{1,0:T(8,128)}) %reduce-scatter.22.cloned.1.call-update) | async-done | bytes 73744
  976.6 104.5 %reduce-scatter.20.cloned.1.call-done = f32[24,768]{1,0:T(8,128)} async-done(((f32[768,768]{1,0:T(8,128)}), f32[24,768]{1,0:T(8,128)}) %reduce-scatter.20.cloned.1.call-update) | async-done | bytes 73744
  1081.2 141.2 %reduce-scatter.18.cloned.1.call-done = f32[96,768]{1,0:T(8,128)} async-done(((f32[3072,768]{1,0:T(8,128)}), f32[96,768]{1,0:T(8,128)}) %reduce-scatter.18.cloned.1.call-update) | async-done | bytes 294928 | tf_op jit(solution)/shard_map/reduce_scatter | solution.py:469
  1222.4 141.7 %reduce-scatter.16.cloned.1.call-done = f32[24,3072]{1,0:T(8,128)} async-done(((f32[768,3072]{1,0:T(8,128)}), f32[24,3072]{1,0:T(8,128)}) %reduce-scatter.16.cloned.1.call-update) | async-done | bytes 294928 | tf_op jit(solution)/shard_map/reduce_scatter | solution.py:468
  (1193 shorter events, 461.9 us)
Async XLA Ops:
  7.2 115.7 %all-gather.8.cloned.1.call-start = ((), (), s32[]{:S(2)}) async-start(), calls=%async_computation.6 | async-start | bytes 1216512 | tf_op jit(solution)/shard_map/all_gather | solution.py:107
  7.9 120.2 %all-gather.10.cloned.1.call-start = ((), (), s32[]{:S(2)}) async-start(), calls=%async_computation.7 | async-start | bytes 1216512 | tf_op jit(solution)/shard_map/all_gather | solution.py:108
  8.7 183.5 %all-gather.12.cloned.1.call-start = ((), (), s32[]{:S(2)}) async-start(), calls=%async_computation.8 | async-start | bytes 1216512 | tf_op jit(solution)/shard_map/all_gather | solution.py:109
  9.4 238.9 %all-gather.14.cloned.1.call-start = ((), (), s32[]{:S(2)}) async-start(), calls=%async_computation.9 | async-start | bytes 1216512 | tf_op jit(solution)/shard_map/all_gather | solution.py:110
  10.0 328.5 %all-gather.16.cloned.1.call-start = ((), (), s32[]{:S(2)}) async-start(), calls=%async_computation.10 | async-start | bytes 4866048 | tf_op jit(solution)/shard_map/all_gather | solution.py:111
  10.6 409.0 %all-gather.18.cloned.1.call-start = ((), (), s32[]{:S(2)}) async-start(), calls=%async_computation.11 | async-start | bytes 4866048 | tf_op jit(solution)/shard_map/all_gather | solution.py:112
  11.2 883.8 %reduce-scatter.14.cloned.1.call-start = ((), (), s32[]{:S(2)}) async-start(), calls=%async_computation.12 | async-start | bytes 2433024 | tf_op jit(solution)/shard_map/reduce_scatter | solution.py:467
  11.2 143.0 %copy-start.279 = (s32[1024]{0:T(1024)}, s32[1024]{0:T(1024)S(1)}, u32[]{:S(2)}) copy-start(s32[1024]{0:T(1024)S(1)} %add_select_fusion) | copy-start | bytes 12292
  12.8 118.6 %copy-start.324 = (pred[1024]{0:T(1024)(128)(4,1)}, pred[1024]{0:T(1024)(128)(4,1)S(1)}, u32[]{:S(2)}) copy-start(pred[1024]{0:T(1024)(128)(4,1)S(1)} %get-tuple-element.145) | copy-start | bytes 3076
  12.8 141.4 %copy-start.322 = (pred[1024]{0:T(1024)(128)(4,1)}, pred[1024]{0:T(1024)(128)(4,1)S(1)}, u32[]{:S(2)}) copy-start(pred[1024]{0:T(1024)(128)(4,1)S(1)} %get-tuple-element.144) | copy-start | bytes 3076
  12.9 270.8 %copy-start.32 = (f32[64,64]{1,0:T(8,128)}, f32[64,64]{1,0:T(8,128)S(1)}, u32[]{:S(2)}) copy-start(f32[64,64]{1,0:T(8,128)S(1)} %fusion.380) | copy-start | bytes 49156
  15.0 116.5 %copy-start.277 = (s32[1,1024]{1,0:T(1,128)}, s32[1,1024]{1,0:T(1,128)S(1)}, u32[]{:S(2)}) copy-start(s32[1,1024]{1,0:T(1,128)S(1)} %get-tuple-element.281) | copy-start | bytes 12292
  15.0 139.3 %copy-start.275 = (s32[1,1024]{1,0:T(1,128)}, s32[1,1024]{1,0:T(1,128)S(1)}, u32[]{:S(2)}) copy-start(s32[1,1024]{1,0:T(1,128)S(1)} %get-tuple-element.280) | copy-start | bytes 12292
  16.7 137.5 %copy-start.326 = (s32[1,64]{1,0:T(1,128)}, s32[1,64]{1,0:T(1,128)S(1)}, u32[]{:S(2)}) copy-start(s32[1,64]{1,0:T(1,128)S(1)} %slice.356) | copy-start | bytes 772
  17.2 114.2 %copy-start.329 = (s32[1,64]{1,0:T(1,128)}, s32[1,64]{1,0:T(1,128)S(1)}, u32[]{:S(2)}) copy-start(s32[1,64]{1,0:T(1,128)S(1)} %slice.394) | copy-start | bytes 772
  19.8 134.5 %copy-start.331 = (pred[64]{0:T(512)(128)(4,1)}, pred[64]{0:T(512)(128)(4,1)S(1)}, u32[]{:S(2)}) copy-start(pred[64]{0:T(512)(128)(4,1)S(1)} %get-tuple-element.312) | copy-start | bytes 196
  20.3 111.2 %copy-start.334 = (pred[64]{0:T(512)(128)(4,1)}, pred[64]{0:T(512)(128)(4,1)S(1)}, u32[]{:S(2)}) copy-start(pred[64]{0:T(512)(128)(4,1)S(1)} %get-tuple-element.313) | copy-start | bytes 196
  20.4 135.4 %copy-start.314 = (pred[64,64]{0,1:T(8,128)(4,1)}, pred[64,64]{0,1:T(8,128)(4,1)S(1)}, u32[]{:S(2)}) copy-start(pred[64,64]{0,1:T(8,128)(4,1)S(1)} %and_and_fusion.3) | copy-start | bytes 12292
  20.5 142.1 %copy-start.115 = (pred[64,1024]{1,0:T(8,128)(4,1)}, pred[64,1024]{1,0:T(8,128)(4,1)S(1)}, u32[]{:S(2)}) copy-start(pred[64,1024]{1,0:T(8,128)(4,1)S(1)} %and_and_fusion.1) | copy-start | bytes 196612
  20.6 124.0 %copy-start.317 = (pred[64,64]{0,1:T(8,128)(4,1)}, pred[64,64]{0,1:T(8,128)(4,1)S(1)}, u32[]{:S(2)}) copy-start(pred[64,64]{0,1:T(8,128)(4,1)S(1)} %and_and_fusion.2) | copy-start | bytes 12292
  20.7 117.2 %copy-start.118 = (pred[64,1024]{1,0:T(8,128)(4,1)}, pred[64,1024]{1,0:T(8,128)(4,1)S(1)}, u32[]{:S(2)}) copy-start(pred[64,1024]{1,0:T(8,128)(4,1)S(1)} %and_and_fusion) | copy-start | bytes 196612
  68.7 246.7 %copy-start.10 = (f32[12,128,160]{1,2,0:T(8,128)}, f32[12,128,160]{1,2,0:T(8,128)S(1)}, u32[]{:S(2)}) copy-start(f32[12,128,160]{1,2,0:T(8,128)S(1)} %copy.704) | copy-start | bytes 2949124
  120.8 111.9 %copy-start.77 = (f32[8,128,160]{1,2,0:T(8,128)}, f32[8,128,160]{1,2,0:T(8,128)S(1)}, u32[]{:S(2)}) copy-start(f32[8,128,160]{1,2,0:T(8,128)S(1)} %and_convert_fusion.1) | copy-start | bytes 1966084
  252.4 81.1 %copy-start.292 = (f32[1024]{0:T(1024)}, f32[1024]{0:T(1024)S(1)}, u32[]{:S(2)}) copy-start(f32[1024]{0:T(1024)S(1)} %broadcast_multiply_fusion.3) | copy-start | bytes 12292
  254.6 79.0 %copy-start.303 = (f32[1024]{0:T(1024)}, f32[1024]{0:T(1024)S(1)}, u32[]{:S(2)}) copy-start(f32[1024]{0:T(1024)S(1)} %fusion.387) | copy-start | bytes 12292
  521.8 81.9 %copy-start.30 = (f32[12,64,1024]{2,1,0:T(8,128)}, f32[12,64,1024]{2,1,0:T(8,128)S(1)}, u32[]{:S(2)}) copy-start(f32[12,64,1024]{2,1,0:T(8,128)S(1)} %fusion.497) | copy-start | bytes 9437188
  668.5 226.5 %reduce-scatter.24.cloned.1.call-start = ((), (), s32[]{:S(2)}) async-start(), calls=%async_computation.17 | async-start | bytes 2433024
  714.3 262.3 %reduce-scatter.22.cloned.1.call-start = ((), (), s32[]{:S(2)}) async-start(), calls=%async_computation.16 | async-start | bytes 2433024
  734.6 346.5 %reduce-scatter.20.cloned.1.call-start = ((), (), s32[]{:S(2)}) async-start(), calls=%async_computation.15 | async-start | bytes 2433024
  759.0 463.3 %reduce-scatter.18.cloned.1.call-start = ((), (), s32[]{:S(2)}) async-start(), calls=%async_computation.14 | async-start | bytes 9732096 | tf_op jit(solution)/shard_map/reduce_scatter | solution.py:469
  778.0 586.1 %reduce-scatter.16.cloned.1.call-start = ((), (), s32[]{:S(2)}) async-start(), calls=%async_computation.13 | async-start | bytes 9732096 | tf_op jit(solution)/shard_map/reduce_scatter | solution.py:468
  839.2 524.9 %copy-start.1 = (bf16[12,33]{1,0:T(8,128)(2,1)S(1)}, bf16[12,33]{1,0:T(8,128)(2,1)}, u32[]{:S(2)}) copy-start(bf16[12,33]{1,0:T(8,128)(2,1)} %param.38) | copy-start | bytes 2380
  (360 other events, 2245.3 us)
Sparse Core Ops, SparseCore 0:
  10.9 56.7 all-gather.7
  70.6 53.0 all-gather.9
  126.6 52.9 all-gather.11
  182.4 52.9 all-gather.13
  238.1 62.5 all-gather.15
  303.5 62.4 all-gather.17
  668.6 99.4 reduce-scatter.13
  774.8 97.8 reduce-scatter.23
  878.6 98.0 reduce-scatter.21
  983.2 97.9 reduce-scatter.19
  1087.6 134.6 reduce-scatter.17
  1229.7 134.3 reduce-scatter.15
where the time goes:
time: 1380 us; the launch traced here: 1370 us
  matrix products  492 us (36%)
  waiting for transfers between devices  473 us (34%)
  local copies, waits for them, and re-layouts  164 us (12%)
  blocking collectives  123 us (9%)
  other arithmetic  97.4 us (7%)
  between operations  20.7 us (2%)
    unnamed x15, waiting for transfers between devices  190 us
    reduce_scatter x1, waiting for transfers between devices, per_device(): lax.psum_scatter(totals[4], ('dp', 'fsdp'), scatter_dimension=0, tiled=True)  142 us
    reduce_scatter x1, waiting for transfers between devices, per_device(): lax.psum_scatter(totals[5], ('dp', 'fsdp'), scatter_dimension=0, tiled=True)  141 us
    unnamed x789, local copies, waits for them, and re-layouts  89.7 us
    unnamed x2, blocking collectives  79.8 us
    dot_general x2, matrix products, forward_pass(): jnp.dot(hidden_low, w_in, preferred_element_type=jnp.float32)  76.6 us
    dot_general x6, matrix products, convolve(): jnp.einsum('bnhir,bnrhe->bnihe', band, value_win, precision=precise)  55.4 us
    dot_general x72, matrix products, newton_pinv(): jnp.einsum('...ij,...jk->...ik', product, bracket, precision=precise)  49.9 us
  transfers between devices with their start and end apart: 12, of which 4 were waited for; matrix products, arithmetic and copies ran while one was open for 34% of the time, Pallas kernels for 0%

commit v1 on v0

v1 whole, which is shorter than its diff:
```python
import functools

import jax
import jax.numpy as jnp
from jax import lax
from jax.experimental import pallas as pl
from jax.experimental.pallas import tpu as pltpu
from jax.sharding import PartitionSpec as P

BF, F32 = jnp.bfloat16, jnp.float32
VMEM_ALL = 67043328
norm_eps = 1e-05


def mm(a, b, dims=((1,), (0,))):
    return lax.dot_general(a, b, (dims, ((), ())), preferred_element_type=F32)


NT = ((1,), (1,))
TN = ((0,), (0,))


def moments(r):
    mean = jnp.mean(r, axis=-1, keepdims=True)
    cent = r - mean
    var = jnp.mean(cent * cent, axis=-1, keepdims=True)
    inv = lax.rsqrt(var + norm_eps)
    return cent * inv, inv


def norm_back(dn, n, inv):
    return (dn - jnp.mean(dn, axis=-1, keepdims=True) - n * jnp.mean(dn * n, axis=-1, keepdims=True)) * inv


def col_sum(v):
    return jnp.sum(v, axis=0, keepdims=True)


def ffn_kernel(x_ref, att_ref, cot_ref, key_ref, wo_ref, wi_ref, wb_ref, vec_ref, bi_ref,
               out_ref, do_ref, datt_ref, gwo_ref, gwi_ref, gwb_ref, gvec_ref, gbi_ref,
               act_s, gp_s, sum_s, hid_s, low_s, *, chunk):
    step = pl.program_id(0)
    inner = wi_ref.shape[1]
    chunks = inner // chunk

    @pl.when(step == 0)
    def _():
        for ref in (gwo_ref, gwi_ref, gwb_ref, gvec_ref, gbi_ref):
            ref[...] = jnp.zeros_like(ref)

    b_out, gain_a, shift_a = vec_ref[2:3, :], vec_ref[3:4, :], vec_ref[4:5, :]
    b_back, gain_f, shift_f = vec_ref[5:6, :], vec_ref[6:7, :], vec_ref[7:8, :]
    r1 = x_ref[...].astype(F32) + (mm(att_ref[...], wo_ref[...]) + b_out)
    n1, inv1 = moments(r1)
    hidden = n1 * gain_a + shift_a
    hid_s[...] = hidden
    low_s[...] = hidden.astype(BF)
    sum_s[...] = jnp.zeros_like(sum_s)

    def up(c, carry):
        cols = pl.ds(pl.multiple_of(c * chunk, chunk), chunk)
        u = mm(low_s[...], wi_ref[:, cols]) + bi_ref[:, cols]
        phi = 0.5 * (1.0 + lax.erf(u * 0.7071067811865476))
        act = (u * phi).astype(BF)
        gp_s[:, cols] = phi + u * (jnp.exp(u * u * -0.5) * 0.3989422804014327)
        act_s[:, cols] = act
        sum_s[...] += mm(act, wb_ref[cols, :])
        return carry

    lax.fori_loop(0, chunks, up, 0)
    n2, inv2 = moments(hid_s[...] + (sum_s[...] + b_back))
    out_ref[...] = (n2 * gain_f + shift_f).astype(BF)
    dy = cot_ref[...].astype(F32)
    gvec_ref[6:7, :] += col_sum(dy * n2)
    gvec_ref[7:8, :] += col_sum(dy)
    dr2 = norm_back(dy * gain_f, n2, inv2)
    df = dr2.astype(BF)
    gvec_ref[5:6, :] += col_sum(df.astype(F32))
    out2 = dr2
    sum_s[...] = out2
    do_ref[...] = df

    def down(c, carry):
        cols = pl.ds(pl.multiple_of(c * chunk, chunk), chunk)
        df = do_ref[...]
        du32 = mm(df, wb_ref[cols, :], NT) * gp_s[:, cols]
        du = du32.astype(BF)
        gwb_ref[cols, :] += mm(act_s[:, cols], df, TN)
        gbi_ref[:, cols] += col_sum(du.astype(F32))
        gwi_ref[:, cols] += mm(low_s[...], du, TN)
        sum_s[...] += mm(du, wi_ref[:, cols], NT)
        return carry

    lax.fori_loop(0, chunks, down, 0)
    dy1 = sum_s[...]
    r1 = x_ref[...].astype(F32) + (mm(att_ref[...], wo_ref[...]) + b_out)
    n1, inv1 = moments(r1)
    gvec_ref[3:4, :] += col_sum(dy1 * n1)
    gvec_ref[4:5, :] += col_sum(dy1)
    do = norm_back(dy1 * gain_a, n1, inv1).astype(BF)
    do_ref[...] = do
    gvec_ref[2:3, :] += col_sum(do.astype(F32))
    gwo_ref[...] += mm(att_ref[...], do, TN)
    live = (key_ref[...] >= 0).astype(F32)
    datt_ref[...] = (mm(do, wo_ref[...], NT) * live).astype(BF)


def ffn(x, att, cot, key_col, wo, wi, wb, vec, bi, tile=512, chunk=768):
    rows, d = x.shape
    inner = wi.shape[1]
    tile = min(tile, rows)
    row = pl.BlockSpec((tile, d), lambda i: (i, 0))
    one = lambda *s: pl.BlockSpec(s, lambda i: tuple(0 for _ in s), pipeline_mode=pl.Buffered(1))
    return pl.pallas_call(
        functools.partial(ffn_kernel, chunk=chunk),
        grid=(rows // tile,),
        in_specs=[row, row, row, pl.BlockSpec((tile, 1), lambda i: (i, 0)), one(d, d), one(d, inner), one(inner, d), one(8, d), one(1, inner)],
        out_specs=[row, row, row, one(d, d), one(d, inner), one(inner, d), one(8, d), one(1, inner)],
        out_shape=[jax.ShapeDtypeStruct((rows, d), BF)] * 3 + [
            jax.ShapeDtypeStruct((d, d), F32), jax.ShapeDtypeStruct((d, inner), F32), jax.ShapeDtypeStruct((inner, d), F32),
            jax.ShapeDtypeStruct((8, d), F32), jax.ShapeDtypeStruct((1, inner), F32)],
        scratch_shapes=[pltpu.VMEM((tile, inner), BF), pltpu.VMEM((tile, inner), F32), pltpu.VMEM((tile, d), F32), pltpu.VMEM((tile, d), F32), pltpu.VMEM((tile, d), BF)],
        compiler_params=pltpu.CompilerParams(vmem_limit_bytes=VMEM_ALL),
        name="ffn",
    )(x, att, cot, key_col, wo, wi, wb, vec, bi)


NEG = -1e30
GW = 256
BLK = 128
WIN = 256


def spread(w, mask):
    return jnp.concatenate([w] * 4, axis=0) * mask


def fold(b, mask):
    b = b * mask
    n = b.shape[0] // 4
    return (b[0:n] + b[n:2 * n]) + (b[2 * n:3 * n] + b[3 * n:4 * n])


def split(w):
    hi = w.astype(BF)
    return hi, (w - hi.astype(F32)).astype(BF)


def dot3(left, right, mask):
    lh, ll = left
    rh, rl = right
    n = lh.shape[0]
    two = mm(jnp.concatenate([lh, ll], axis=0), spread(rh, mask))
    return two[:n] + (two[n:] + mm(lh, spread(rl, mask)))


def head_swap(w):
    t = w.T
    n = w.shape[0]
    parts = [t[h * n:(h + 1) * n, :] for h in range(4)]
    return jnp.concatenate(parts, axis=1)


def lane_group(shape):
    return lax.broadcasted_iota(jnp.int32, shape, 1) // 64


def attn_fwd_kernel(x_ref, wq_ref, wk_ref, wv_ref, vec_ref, keyc_ref, keyr_ref, kwin_ref, lkc_ref, lkr_ref, cw_ref,
                    q_ref, k_ref, v_ref, lq_ref, lk_ref, fm_ref, bm_ref, at_ref, aw_ref, fro_ref,
                    zs_ref, ps_ref, b2_ref, b3_ref, zf_ref, sw_ref, g_ref, att_ref,
                    sc_s, cv_s, tap_s, z_s, *, seqs, length, land, taps):
    d = x_ref.shape[1]
    groups = d // GW
    n = seqs * groups
    stride = length // land
    half = taps // 2
    heads = d // 64
    scale = 0.125
    mask32 = (lax.broadcasted_iota(jnp.int32, (GW, GW), 0) // 64 == lax.broadcasted_iota(jnp.int32, (GW, GW), 1) // 64).astype(F32)
    mask = mask32.astype(BF)
    eye = (lax.broadcasted_iota(jnp.int32, (64, GW), 0) == lax.broadcasted_iota(jnp.int32, (64, GW), 1) % 64).astype(F32)

    def project(b, carry):
        rows = pl.ds(pl.multiple_of(b * length, length), length)
        xb = x_ref[rows, :]
        q_ref[rows, :] = (mm(xb, wq_ref[...]) + vec_ref[0:1, :]).astype(BF)
        k_ref[rows, :] = mm(xb, wk_ref[...]).astype(BF)
        v_ref[b, 0:half, :] = jnp.zeros((half, d), BF)
        v_ref[b, length + half:, :] = jnp.zeros((v_ref.shape[1] - length - half, d), BF)
        v_ref[b, half:half + length, :] = (mm(xb, wv_ref[...]) + vec_ref[1:2, :]).astype(BF)
        lrows = pl.ds(pl.multiple_of(b * land, land), land)
        member = ((lax.broadcasted_iota(jnp.int32, (land, length), 1) // stride == lax.broadcasted_iota(jnp.int32, (land, length), 0))
                  & (lkc_ref[lrows, :] == keyr_ref[b])).astype(F32)
        count = jnp.maximum(jnp.sum(member, axis=1, keepdims=True), 1.0)
        memb = member.astype(BF)
        lq_ref[lrows, :] = (mm(memb, q_ref[rows, :]) / count).astype(BF)
        lk_ref[lrows, :] = (mm(memb, k_ref[rows, :]) / count).astype(BF)
        return carry

    lax.fori_loop(0, seqs, project, 0)

    for h in range(heads):
        tap_s[h * BLK:(h + 1) * BLK, :] = pltpu.roll(
            jnp.broadcast_to(cw_ref[h:h + 1, :], (BLK, WIN)), 0, 1, stride=1, stride_axis=0).astype(BF)

    def scores(i, carry):
        b, g = i // groups, i % groups
        rows = pl.ds(pl.multiple_of(b * length, length), length)
        lrows = pl.ds(pl.multiple_of(b * land, land), land)
        cols = pl.ds(pl.multiple_of(g * GW, GW), GW)
        lq, lk = lq_ref[lrows, cols], lk_ref[lrows, cols]
        lqb, lkb = spread(lq, mask), spread(lk, mask)
        lkc, keyr = lkc_ref[lrows, :], keyr_ref[b]
        sc_s[...] = mm(lkb, q_ref[rows, cols], NT)
        half_l = length // 2
        for h in range(4):
            for t in range(2):
                tc = slice(t * half_l, (t + 1) * half_l)
                ok = lkc == keyr[:, tc]
                s = jnp.where(ok, sc_s[h * 64:(h + 1) * 64, tc] * scale, NEG)
                e = jnp.exp(s - jnp.max(s, axis=0, keepdims=True))
                fm_ref[i, h * 64:(h + 1) * 64, tc] = (e / jnp.sum(e, axis=0, keepdims=True)).astype(BF)
        sc_s[...] = mm(lqb, k_ref[rows, cols], NT)
        for h in range(4):
            for t in range(2):
                jr = slice(t * 32, (t + 1) * 32)
                ok = lkc[jr] == keyr
                s = jnp.where(ok, sc_s[h * 64 + t * 32:h * 64 + (t + 1) * 32, :] * scale, NEG)
                e = jnp.exp(s - jnp.max(s, axis=1, keepdims=True))
                live = (lkc[jr] >= 0).astype(F32)
                bm_ref[i, h * 64 + t * 32:h * 64 + (t + 1) * 32, :] = (e / jnp.sum(e, axis=1, keepdims=True) * live).astype(BF)
        vg = v_ref[b, half:half + length, cols]
        sw_ref[i] = fold(mm(bm_ref[i], vg), mask32)
        lkr = lkr_ref[b]
        s = jnp.where(lkc == lkr, mm(lk, lqb, NT) * scale, NEG)
        e = jnp.exp(s - jnp.max(s, axis=0, keepdims=True))
        at = e / jnp.sum(e, axis=0, keepdims=True) * (lkr >= 0).astype(F32)
        at_ref[i] = at
        aw_ref[i] = head_swap(at)
        cs = jnp.sum(at * at, axis=0, keepdims=True)
        lg = lane_group((1, GW))
        fro = jnp.zeros((1, GW), F32)
        for h in range(4):
            fro += jnp.where(lg == h, jnp.sum(jnp.where(lg == h, cs, 0.0), axis=1, keepdims=True), 0.0)
        fro = fro + 1e-6
        fro_ref[i] = fro
        z_s[i] = at / fro
        return carry

    lax.fori_loop(0, n, scores, 0)

    steps = zs_ref.shape[0]
    blocks = length // BLK
    per = -(-(seqs * blocks) // steps)

    def newton(step, carry):
        al, zl, pl_, b1, b2, b3 = ([None] * n for _ in range(6))
        for i in range(n):
            z = z_s[i]
            al[i], zl[i] = split(aw_ref[i]), split(z)
            zs_ref[step, i] = zl[i][0]
        for i in range(n):
            p = dot3(al[i], zl[i], mask)
            pl_[i] = split(p)
            ps_ref[step, i] = pl_[i][0]
            b1[i] = split(7.0 * eye - p)
        for i in range(n):
            v = 15.0 * eye - dot3(pl_[i], b1[i], mask)
            b2[i] = split(v)
            b2_ref[step, i] = b2[i][0]
        for i in range(n):
            v = 13.0 * eye - dot3(pl_[i], b2[i], mask)
            b3[i] = split(v)
            b3_ref[step, i] = b3[i][0]
        for i in range(n):
            z_s[i] = 0.25 * dot3(zl[i], b3[i], mask)

        def conv(m, c2):
            e = jnp.minimum(step * per + m, seqs * blocks - 1)
            b, blk = e // blocks, e % blocks
            trow = pl.ds(pl.multiple_of(e * BLK, BLK), BLK)
            kept = (keyc_ref[trow, :] == kwin_ref[e]).astype(F32).astype(BF)
            kept4 = jnp.concatenate([kept] * 4, axis=0)
            lg = lane_group((BLK, GW))
            for g in range(groups):
                band = tap_s[g * 4 * BLK:(g + 1) * 4 * BLK, :] * kept4
                y = mm(band, v_ref[b, pl.ds(pl.multiple_of(blk * BLK, BLK), WIN), g * GW:(g + 1) * GW])
                r = jnp.where(lg < 2, jnp.where(lg == 0, y[:BLK], y[BLK:2 * BLK]), jnp.where(lg == 2, y[2 * BLK:3 * BLK], y[3 * BLK:]))
                cv_s[trow, g * GW:(g + 1) * GW] = r
            return c2

        lax.fori_loop(0, per, conv, 0)
        return carry

    lax.fori_loop(0, steps, newton, 0)

    def finish(i, carry):
        b, g = i // groups, i % groups
        rows = pl.ds(pl.multiple_of(b * length, length), length)
        cols = pl.ds(pl.multiple_of(g * GW, GW), GW)
        z = z_s[i]
        zf_ref[i] = z
        gl = dot3(split(z), split(sw_ref[i]), mask).astype(BF)
        g_ref[i] = gl
        y = mm(fm_ref[i], spread(gl, mask), TN) + cv_s[rows, cols]
        att_ref[rows, cols] = jnp.where(keyc_ref[rows, :] >= 0, y, 0.0).astype(BF)
        return carry

    lax.fori_loop(0, n, finish, 0)


def vm(k):
    return [pl.BlockSpec(memory_space=pltpu.VMEM)] * k


def attn_fwd(x, wq, wk, wv, vec, keys, cw, seqs, land, taps, steps):
    keyc, keyr, kwin, lkc, lkr = keys
    rows, d = x.shape
    length = rows // seqs
    n = seqs * (d // GW)
    S = jax.ShapeDtypeStruct
    vrows = length - BLK + WIN
    outs = dict(
        q=S((rows, d), BF), k=S((rows, d), BF), v=S((seqs, vrows, d), BF), lq=S((seqs * land, d), BF), lk=S((seqs * land, d), BF),
        fm=S((n, GW, length), BF), bm=S((n, GW, length), BF), at=S((n, 64, GW), F32), aw=S((n, 64, GW), F32), fro=S((n, 1, GW), F32),
        zs=S((steps, n, 64, GW), BF), ps=S((steps, n, 64, GW), BF), b2=S((steps, n, 64, GW), BF), b3=S((steps, n, 64, GW), BF),
        zf=S((n, 64, GW), F32), sw=S((n, 64, GW), F32), g=S((n, 64, GW), BF), att=S((rows, d), BF))
    res = pl.pallas_call(
        functools.partial(attn_fwd_kernel, seqs=seqs, length=length, land=land, taps=taps),
        in_specs=vm(11), out_specs=vm(len(outs)), out_shape=list(outs.values()),
        scratch_shapes=[pltpu.VMEM((GW, length), F32), pltpu.VMEM((rows, d), F32), pltpu.VMEM((d // 64 * BLK, WIN), BF), pltpu.VMEM((n, 64, GW), F32)],
        compiler_params=pltpu.CompilerParams(vmem_limit_bytes=VMEM_ALL),
        name="attn_fwd",
    )(x, wq, wk, wv, vec, keyc, keyr, kwin, lkc, lkr, cw)
    return dict(zip(outs, res))


def make_keys(seg, pad, land, taps):
    seqs, length = seg.shape
    stride = length // land
    half = taps // 2
    live = pad == 1
    key = jnp.where(live, seg, -2)
    keyc = key.reshape(seqs * length, 1)
    keyr = key.reshape(seqs, 1, length)
    keyw = jnp.pad(jnp.where(live, seg, -1), ((0, 0), (half, WIN - BLK - half)), constant_values=-1)
    blocks = length // BLK
    kwin = jnp.stack([keyw[:, b * BLK:b * BLK + WIN] for b in range(blocks)], axis=1).reshape(seqs * blocks, 1, WIN)
    lead = jnp.where(live, seg, -1)[:, ::stride]
    lkc = lead.reshape(seqs * land, 1)
    lkr = jnp.tile(jnp.where(lead >= 0, lead, -3), (1, 4)).reshape(seqs, 1, 4 * land)
    return keyc, keyr, kwin, lkc, lkr


def make_taps(cw):
    heads, taps = cw.shape
    w = cw.astype(F32)
    return jnp.pad(w, ((0, 0), (0, WIN - taps))), jnp.pad(w[:, ::-1], ((0, 0), (0, WIN - taps)))


def attn_bwd_kernel(datt_ref, q_ref, k_ref, v_ref, lq_ref, lk_ref, fm_ref, bm_ref, at_ref, aw_ref, fro_ref,
                    zs_ref, ps_ref, b2_ref, b3_ref, zf_ref, sw_ref, g_ref,
                    keyc_ref, keyr_ref, kwin_ref, lkc_ref, cw_ref,
                    dq_ref, dk_ref, dv_ref, gc_ref,
                    sc_s, dp_s, tap_s, dsf_s, dsb_s, dv_s, d_s, da_s, dlq_s, dlk_s, x_s, *, seqs, length, land, taps):
    d = q_ref.shape[1]
    groups = d // GW
    n = seqs * groups
    stride = length // land
    half = taps // 2
    heads = d // 64
    scale = 0.125
    mask32 = (lax.broadcasted_iota(jnp.int32, (GW, GW), 0) // 64 == lax.broadcasted_iota(jnp.int32, (GW, GW), 1) // 64).astype(F32)
    mask = mask32.astype(BF)
    eye = (lax.broadcasted_iota(jnp.int32, (64, GW), 0) == lax.broadcasted_iota(jnp.int32, (64, GW), 1) % 64).astype(F32)

    for h in range(heads):
        tap_s[h * BLK:(h + 1) * BLK, :] = pltpu.roll(
            jnp.broadcast_to(cw_ref[h:h + 1, :], (BLK, WIN)), 0, 1, stride=1, stride_axis=0).astype(BF)
    for b in range(seqs):
        dp_s[b, 0:half, :] = jnp.zeros((half, d), BF)
        dp_s[b, half:half + length, :] = datt_ref[b * length:(b + 1) * length, :]
        dp_s[b, half + length:, :] = jnp.zeros((dp_s.shape[1] - length - half, d), BF)
    x_s[...] = jnp.zeros_like(x_s)

    def outer(i, carry):
        b, g = i // groups, i % groups
        rows = pl.ds(pl.multiple_of(b * length, length), length)
        cols = pl.ds(pl.multiple_of(g * GW, GW), GW)
        dg4 = datt_ref[rows, cols]
        sc_s[...] = mm(spread(g_ref[i], mask), dg4, NT)
        half_l = length // 2
        for h in range(4):
            for t in range(2):
                hr, tc = slice(h * 64, (h + 1) * 64), slice(t * half_l, (t + 1) * half_l)
                p, dp = fm_ref[i, hr, tc].astype(F32), sc_s[hr, tc]
                dsf_s[i, hr, tc] = (p * (dp - jnp.sum(dp * p, axis=0, keepdims=True))).astype(BF)
        gbd = mm(fm_ref[i], dg4) * mask32
        gh, gl = split(gbd)
        zh, zl = split(zf_ref[i])
        zh, zl = spread(zh, mask), spread(zl, mask)
        dsb = (mm(zh, gh, TN) + (mm(zl, gh, TN) + mm(zh, gl, TN))).astype(BF)
        d_s[i] = mm(sw_ref[i].astype(BF), gh, NT)
        da_s[i] = jnp.zeros((64, GW), F32)
        sc_s[...] = mm(dsb, v_ref[b, half:half + length, cols], NT)
        for h in range(8):
            hr = slice(h * 32, (h + 1) * 32)
            p, dp = bm_ref[i, hr, :].astype(F32), sc_s[hr, :]
            dsb_s[i, hr, :] = (p * (dp - jnp.sum(dp * p, axis=1, keepdims=True))).astype(BF)
        dv_s[rows, cols] = mm(bm_ref[i], dsb, TN)
        dlq_s[i] = fold(mm(dsb_s[i], k_ref[rows, cols]), mask32)
        dlk_s[i] = fold(mm(dsf_s[i], q_ref[rows, cols]), mask32)
        return carry

    lax.fori_loop(0, n, outer, 0)

    steps = zs_ref.shape[0]
    blocks = length // BLK
    per = -(-(seqs * blocks) // steps)

    def newton(r, carry):
        s = steps - 1 - r
        dl, db3, dp, db2, dz = ([None] * n for _ in range(5))
        for i in range(n):
            dl[i] = d_s[i].astype(BF)
        for i in range(n):
            db3[i] = (0.25 * mm(dl[i], spread(zs_ref[s, i], mask))).astype(BF)
            dz[i] = 0.25 * mm(b3_ref[s, i], spread(dl[i], mask))
        for i in range(n):
            dp[i] = mm(b2_ref[s, i], spread(db3[i], mask))
            db2[i] = (-mm(db3[i], spread(ps_ref[s, i], mask))).astype(BF)
        for i in range(n):
            p = ps_ref[s, i]
            b1 = (7.0 * eye - p.astype(F32)).astype(BF)
            dp[i] = dp[i] + mm(b1, spread(db2[i], mask)) - mm(db2[i], spread(p, mask))
            dp[i] = (-dp[i]).astype(BF)
        for i in range(n):
            da_s[i] += mm(zs_ref[s, i], spread(dp[i], mask))
            d_s[i] = dz[i] + mm(dp[i], spread(aw_ref[i].astype(BF), mask))

        def conv(m, c2):
            e = r * per + m

            @pl.when(e < seqs * blocks)
            def _():
                b, blk = e // blocks, e % blocks
                t0 = pl.multiple_of(blk * BLK, BLK)
                trow = pl.ds(pl.multiple_of(e * BLK, BLK), BLK)
                kept = (keyc_ref[trow, :] == kwin_ref[e]).astype(F32)
                kept4 = jnp.concatenate([kept.astype(BF)] * 4, axis=0)
                lg = lane_group((BLK, GW))
                for g in range(groups):
                    gc = slice(g * GW, (g + 1) * GW)
                    band = tap_s[g * 4 * BLK:(g + 1) * 4 * BLK, :] * kept4
                    y = mm(band, dp_s[b, pl.ds(t0, WIN), gc])
                    r4 = jnp.where(lg < 2, jnp.where(lg == 0, y[:BLK], y[BLK:2 * BLK]), jnp.where(lg == 2, y[2 * BLK:3 * BLK], y[3 * BLK:]))
                    dv_s[trow, gc] += r4
                    own = datt_ref[trow, gc]
                    four = jnp.concatenate([own * (lg == h).astype(F32).astype(BF) for h in range(4)], axis=0)
                    y = mm(four, v_ref[b, pl.ds(t0, WIN), gc], NT)
                    for h in range(4):
                        x_s[(g * 4 + h) * BLK:(g * 4 + h + 1) * BLK, :] += y[h * BLK:(h + 1) * BLK] * kept
            return c2

        lax.fori_loop(0, per, conv, 0)
        return carry

    lax.fori_loop(0, steps, newton, 0)

    ri = lax.broadcasted_iota(jnp.int32, (BLK, WIN), 0)
    for h in range(heads):
        v = x_s[h * BLK:(h + 1) * BLK, :]
        bit = 1
        while bit < BLK:
            v = jnp.where((ri & bit) != 0, pltpu.roll(v, WIN - bit, 1), v)
            bit *= 2
        gc_ref[h:h + 1, :] = jnp.sum(v, axis=0, keepdims=True)

    def finish(i, carry):
        b, g = i // groups, i % groups
        rows = pl.ds(pl.multiple_of(b * length, length), length)
        lrows = pl.ds(pl.multiple_of(b * land, land), land)
        cols = pl.ds(pl.multiple_of(g * GW, GW), GW)
        fro, at, aw, d0 = fro_ref[i], at_ref[i], aw_ref[i], d_s[i]
        cs = jnp.sum(d0 * aw, axis=0, keepdims=True)
        lg = lane_group((1, GW))
        tot = jnp.zeros((1, GW), F32)
        for h in range(4):
            tot += jnp.where(lg == h, jnp.sum(jnp.where(lg == h, cs, 0.0), axis=1, keepdims=True), 0.0)
        da = da_s[i] + head_swap(d0 / fro) - (2.0 * tot / (fro * fro)) * at
        dsa = (at * (da - jnp.sum(da * at, axis=0, keepdims=True))).astype(BF)
        lqb, lkb = spread(lq_ref[lrows, cols], mask), spread(lk_ref[lrows, cols], mask)
        member = ((lax.broadcasted_iota(jnp.int32, (land, length), 1) // stride == lax.broadcasted_iota(jnp.int32, (land, length), 0))
                  & (lkc_ref[lrows, :] == keyr_ref[b])).astype(F32)
        count = jnp.maximum(jnp.sum(member, axis=1, keepdims=True), 1.0)
        memb = member.astype(BF)
        dlk = (dlk_s[i] + mm(dsa, lqb)) * scale / count
        dlq = (dlq_s[i] + fold(mm(spread(dsa, mask), lkb, TN), mask32)) * scale / count
        yh, yl = split(dlq)
        dq_ref[rows, cols] = mm(jnp.concatenate([dsf_s[i], memb, memb], axis=0), jnp.concatenate([lkb * scale, yh, yl], axis=0), TN).astype(BF)
        yh, yl = split(dlk)
        dk_ref[rows, cols] = mm(jnp.concatenate([dsb_s[i], memb, memb], axis=0), jnp.concatenate([lqb * scale, yh, yl], axis=0), TN).astype(BF)
        dv_ref[rows, cols] = dv_s[rows, cols].astype(BF)
        return carry

    lax.fori_loop(0, n, finish, 0)


def attn_bwd(datt, sv, keys, cwb, seqs, land, taps):
    keyc, keyr, kwin, lkc, lkr = keys
    rows, d = datt.shape
    length = rows // seqs
    n = seqs * (d // GW)
    heads = d // 64
    S = jax.ShapeDtypeStruct
    V = pltpu.VMEM
    vrows = length - BLK + WIN
    names = ("q", "k", "v", "lq", "lk", "fm", "bm", "at", "aw", "fro", "zs", "ps", "b2", "b3", "zf", "sw", "g")
    return pl.pallas_call(
        functools.partial(attn_bwd_kernel, seqs=seqs, length=length, land=land, taps=taps),
        in_specs=vm(1 + len(names) + 5), out_specs=vm(4),
        out_shape=[S((rows, d), BF)] * 3 + [S((heads, WIN), F32)],
        scratch_shapes=[V((GW, length), F32), V((seqs, vrows, d), BF), V((heads * BLK, WIN), BF), V((n, GW, length), BF), V((n, GW, length), BF),
                        V((rows, d), F32)] + [V((n, 64, GW), F32)] * 4 + [V((heads * BLK, WIN), F32)],
        compiler_params=pltpu.CompilerParams(vmem_limit_bytes=VMEM_ALL),
        name="attn_bwd",
    )(datt, *[sv[k] for k in names], keyc, keyr, kwin, lkc, cwb)


def proj_kernel(x_ref, do_ref, dq_ref, dk_ref, dv_ref, wq_ref, wk_ref, wv_ref, gt_ref, gwq_ref, gwk_ref, gwv_ref, gb_ref):
    @pl.when(pl.program_id(0) == 0)
    def _():
        for ref in (gwq_ref, gwk_ref, gwv_ref, gb_ref):
            ref[...] = jnp.zeros_like(ref)

    x = x_ref[...]
    gwq_ref[...] += mm(x, dq_ref[...], TN)
    gwk_ref[...] += mm(x, dk_ref[...], TN)
    gwv_ref[...] += mm(x, dv_ref[...], TN)
    gb_ref[0:1, :] += col_sum(dq_ref[...].astype(F32))
    gb_ref[1:2, :] += col_sum(dv_ref[...].astype(F32))
    gt = do_ref[...].astype(F32) + mm(dq_ref[...], wq_ref[...], NT)
    gt = gt + mm(dk_ref[...], wk_ref[...], NT)
    gt_ref[...] = (gt + mm(dv_ref[...], wv_ref[...], NT)).astype(BF)


def proj_bwd(x, do, dq, dk, dv, wq, wk, wv, tile=1024):
    rows, d = x.shape
    tile = min(tile, rows)
    row = pl.BlockSpec((tile, d), lambda i: (i, 0))
    one = lambda *s: pl.BlockSpec(s, lambda i: tuple(0 for _ in s), pipeline_mode=pl.Buffered(1))
    S = jax.ShapeDtypeStruct
    return pl.pallas_call(
        proj_kernel, grid=(rows // tile,),
        in_specs=[row] * 5 + [one(d, d)] * 3,
        out_specs=[row] + [one(d, d)] * 3 + [one(8, d)],
        out_shape=[S((rows, d), BF)] + [S((d, d), F32)] * 3 + [S((8, d), F32)],
        compiler_params=pltpu.CompilerParams(vmem_limit_bytes=VMEM_ALL),
        name="proj_bwd",
    )(x, do, dq, dk, dv, wq, wk, wv)


AXES = ("dp", "fsdp")
LAND = 64
PINV_STEPS = 6


def per_device(tokens, seg_ids, pad_mask, w_query, w_key, w_value, w_out, w_in, w_back, b_query, b_value, b_out,
               gain_attn, shift_attn, b_in, b_back, gain_ffn, shift_ffn, conv_weight, cotangent):
    seqs, length, d = tokens.shape
    taps = conv_weight.shape[1]
    part = w_query.shape[0]
    inner = w_in.shape[1]
    small = jnp.concatenate([b_query, b_value, b_out, gain_attn, shift_attn, b_back, gain_ffn, shift_ffn, b_in])
    pad_rows = -(-small.shape[0] // d)
    small = jnp.pad(small, (0, pad_rows * d - small.shape[0])).reshape(pad_rows, d)
    first = lax.all_gather(jnp.concatenate([w_query, w_key, w_value, small], axis=0)[None], AXES, axis=0, tiled=True)
    ffw = jnp.concatenate([w_in[:, c * d:(c + 1) * d] for c in range(inner // d)], axis=0)
    second = lax.all_gather(jnp.concatenate([w_out, ffw, w_back], axis=0)[None], AXES, axis=0, tiled=True)
    n = first.shape[0]
    take = lambda s, k: s[:, k * part:(k + 1) * part].reshape(n * part, d)
    wq, wk, wv = (take(first, k) for k in range(3))
    small = first[:, 3 * part:].reshape(n, -1)
    vec = small[:, :8 * part].reshape(n, 8, part).transpose(1, 0, 2).reshape(8, n * part).astype(F32)
    bi = small[:, 8 * part:8 * part + inner // n].reshape(1, inner).astype(F32)
    wo = take(second, 0)
    wi = jnp.concatenate([take(second, 1 + c) for c in range(inner // d)], axis=1)
    wb = second[:, (1 + inner // d) * part:].reshape(inner, d)

    keys = make_keys(seg_ids, pad_mask, LAND, taps)
    taps_f, taps_b = make_taps(conv_weight)
    x = tokens.reshape(-1, d)
    sv = attn_fwd(x, wq, wk, wv, vec, keys, taps_f, seqs, LAND, taps, PINV_STEPS)
    out, do, datt, gwo, gwi, gwb, gvec, gbi = ffn(x, sv["att"], cotangent.reshape(-1, d), keys[0], wo, wi, wb, vec, bi, 512, 1024)
    split_rows = lambda g: g.astype(BF).reshape(n, -1, d)
    gi = jnp.concatenate([gwi[:, c * d:(c + 1) * d].astype(BF).reshape(n, part, d) for c in range(inner // d)], axis=1)
    late = lax.psum_scatter(jnp.concatenate([split_rows(gwo), gi, split_rows(gwb)], axis=1), AXES, scatter_dimension=0, tiled=True)[0].astype(F32)
    dq, dk, dv, gc = attn_bwd(datt, sv, keys, taps_b, seqs, LAND, taps)
    gt, gwq, gwk, gwv, gb = proj_bwd(x, do, dq, dk, dv, wq, wk, wv)
    last = lax.psum_scatter(jnp.concatenate([split_rows(gwq), split_rows(gwk), split_rows(gwv)], axis=1), AXES, scatter_dimension=0, tiled=True)[0].astype(F32)
    gvec = jnp.concatenate([gb[:2], gvec[2:]], axis=0)
    gvec, gbi, gc = lax.psum((gvec, gbi, gc), AXES)
    me = lax.axis_index(AXES)
    vs = lax.dynamic_slice(gvec, (0, me * part), (8, part))
    bs = lax.dynamic_slice(gbi[0], (me * (inner // n),), (inner // n,))
    go = late[:part]
    gi = jnp.concatenate([late[(1 + c) * part:(2 + c) * part] for c in range(inner // d)], axis=1)
    gbk = late[(1 + inner // d) * part:]
    return (out.reshape(tokens.shape), gt.reshape(tokens.shape), last[:part], last[part:2 * part], last[2 * part:], go, gi, gbk,
            vs[0], vs[1], vs[2], vs[3], vs[4], bs, vs[5], vs[6], vs[7], gc[:, :taps])


def solution(mesh):
    rows = P(AXES, None)
    seq = P(AXES, None, None)
    vector = P(AXES)
    in_specs = (seq, rows, rows) + (rows,) * 6 + (vector,) * 9 + (P(), seq)
    out_specs = (seq, seq) + (rows,) * 6 + (vector,) * 9 + (P(),)
    return jax.shard_map(per_device, mesh=mesh, in_specs=in_specs, out_specs=out_specs, check_vma=False)
```

time: 1380 us -> 634 us (0.46)
  matrix products: 492 us -> 0 us
  Pallas kernels: 0 us -> 232 us
  waiting for transfers between devices: 473 us -> 270 us
  local copies, waits for them, and re-layouts: 164 us -> 52 us
  blocking collectives: 123 us -> 40 us
  other arithmetic: 97.4 us -> 17.7 us
    dot_general x229 -> x0, matrix products: 485 us -> none  [the longest x2 76.6 us: forward_pass(): jnp.dot(hidden_low, w_in, preferred_element_type=jnp.float32)]
    pallas_call x0 -> x4, Pallas kernels: none -> 232 us  [the longest x1 105 us: ffn(): pl.pallas_call(functools.partial(ffn_kernel, chunk=chunk), grid=(rows //...]
    unnamed x15 -> x4, waiting for transfers between devices: 190 us -> 0.07 us
    reduce_scatter x3 -> x2, waiting for transfers between devices: 283 us -> 186 us  [the longest x1 145 us: per_device(): lax.psum_scatter(jnp.concatenate([split_rows(gwo), gi, split_rows(gwb)],...]
    all_gather x6 -> x2, waiting for transfers between devices: 0.07 us -> 83.6 us  [the longest x1 50.2 us: per_device(): lax.all_gather(jnp.concatenate([w_query, w_key, w_value, small], axis=0)[...]
    unnamed x2 -> x0, blocking collectives: 79.8 us -> none
    unnamed x789 -> x40, local copies, waits for them, and re-layouts: 89.7 us -> 16.5 us
    reduce_sum x25 -> x0, other arithmetic: 61.4 us -> none  [the longest x3 19.3 us: masked_softmax(): exp_terms = jnp.exp(held_scores - row_top)]
  transfers between devices with their start and end apart: 12 -> 4, of which waited for: 4 -> 4; matrix products, arithmetic and copies ran while one was open for 34% -> 6% of each run, Pallas kernels for 0% -> 8%
where the time goes in v1:
time: 634 us; the launch traced here: 626 us
  waiting for transfers between devices  270 us (43%)
  Pallas kernels  232 us (37%)
  local copies, waits for them, and re-layouts  52 us (8%)
  blocking collectives  40 us (6%)
  other arithmetic  17.7 us (3%)
  between operations  14.4 us (2%)
    reduce_scatter x1, waiting for transfers between devices, per_device(): lax.psum_scatter(jnp.concatenate([split_rows(gwo), gi, split_rows(gwb)],...  145 us
    pallas_call x1, Pallas kernels, ffn(): pl.pallas_call(functools.partial(ffn_kernel, chunk=chunk), grid=(rows //...  105 us
    pallas_call x1, Pallas kernels, attn_bwd(): pl.pallas_call(functools.partial(attn_bwd_kernel, seqs=seqs, length=lengt...  54.5 us
    all_gather x1, waiting for transfers between devices, per_device(): lax.all_gather(jnp.concatenate([w_query, w_key, w_value, small], axis=0)[...  50.2 us
    pallas_call x1, Pallas kernels, attn_fwd(): pl.pallas_call(functools.partial(attn_fwd_kernel, seqs=seqs, length=lengt...  49.4 us
    reduce_scatter x1, waiting for transfers between devices, per_device(): lax.psum_scatter(jnp.concatenate([split_rows(gwq), split_rows(gwk), split...  41.3 us
    psum x1, blocking collectives, per_device(): gvec, gbi, gc = lax.psum((gvec, gbi, gc), AXES)  40 us
    all_gather x1, waiting for transfers between devices, per_device(): lax.all_gather(jnp.concatenate([w_out, ffw, w_back], axis=0)[None], AXES,...  33.4 us
  transfers between devices with their start and end apart: 4, of which 4 were waited for; matrix products, arithmetic and copies ran while one was open for 6% of the time, Pallas kernels for 8%

profile of v1, /device:TPU:0, one launch (start us, length us, event | category | flops | bytes accessed | tf_op | source)
XLA Modules:
  0.0 626.2 jit_solution(14192046808563303226)
XLA Ops:
  7.2 6.1 concatenate.24
  13.4 1.5 maximum_bitcast_fusion
  18.8 0.9 constant_dynamic-update-slice_fusion.8
  24.7 1.3 copy.72
  26.8 1.3 pad.17.cw_ref
  28.7 50.2 %all-gather.8.cloned.1.call-done = bf16[32,73,768]{2,1,0:T(8,128)(2,1)} async-done(((bf16[1,73,768]{2,1,0:T(8,128)(2,1)}), bf16[32,73,768]{2,1,0:T(8,128)(2,1)}) %all-gather.8.cloned.1.call-update) | async-done | bytes 3588112 | tf_op jit(solution)/shard_map/all_gather | solution.py:577
  78.9 1.0 slice.245
  81.6 3.8 fusion.4
  85.4 49.4 %attn_fwd.1 = (bf16[2048,768]{1,0:T(8,128)(2,1)}, bf16[2048,768]{1,0:T(8,128)(2,1)}, bf16[2,1152,768]{2,1,0:T(8,128)(2,1)}, bf16[128,768]{1,0:T(8,128)(2,1)}, bf...) custom-call(bf16[2048,768]{1,0:T(8,128)(2,1)} %bitcast.101, ...), custom_call_target="tpu_custom_call" | custom-call | tf_op jit(solution)/shard_map/attn_fwd/pallas_call | solution.py:328
  134.8 33.4 %all-gather.6.cloned.1.call-done = bf16[6912,768]{1,0:T(8,128)(2,1)} async-done(((bf16[216,768]{1,0:T(8,128)(2,1)}), bf16[6912,768]{1,0:T(8,128)(2,1)}) %all-gather.6.cloned.1.call-update) | async-done | bytes 10616848 | tf_op jit(solution)/shard_map/all_gather | solution.py:579
  168.2 4.1 fusion.2
  172.3 4.8 slice.258
  177.1 2.5 pad_maximum_fusion.wi_ref
  179.6 105.2 %ffn.1 = (bf16[2048,768]{1,0:T(8,128)(2,1)}, bf16[2048,768]{1,0:T(8,128)(2,1)}, bf16[2048,768]{1,0:T(8,128)(2,1)}, f32[768,768]{1,0:T(8,128)}, f32[768,3072]{1,0...) custom-call(bf16[2048,768]{1,0:T(8,128)(2,1)} %bitcast.102, ...), custom_call_target="tpu_custom_call" | custom-call | tf_op jit(solution)/shard_map/ffn/pallas_call | solution.py:114
  284.8 54.5 %attn_bwd.1 = (bf16[2048,768]{1,0:T(8,128)(2,1)}, bf16[2048,768]{1,0:T(8,128)(2,1)}, bf16[2048,768]{1,0:T(8,128)(2,1)}, f32[12,256]{1,0:T(8,128)}) custom-call(bf16[2048,768]{1,0:T(8,128)(2,1)} %get-tuple-element.56.datt_ref, bf16[2048,768]{1,0:T(8,128)(2,1)} %get-tuple-element.57.q_ref, bf16[2048,768]{1,0:T(8,128)(2,1)} %get-tuple-element.58.k_ref, ...), custom_call_target="tpu_custom_call" | custom-call | tf_op jit(solution)/shard_map/attn_bwd/pallas_call | solution.py:519
  339.3 22.7 %proj_bwd.1 = (bf16[2048,768]{1,0:T(8,128)(2,1)}, f32[768,768]{1,0:T(8,128)}, f32[768,768]{1,0:T(8,128)}, f32[768,768]{1,0:T(8,128)}, f32[8,768]{1,0:T(8,128)}) custom-call(bf16[2048,768]{1,0:T(8,128)(2,1)} %bitcast.103, bf16[2048,768]{1,0:T(8,128)(2,1)} %get-tuple-element.55.do_ref, bf16[2048,768]{1,0:T(8,128)(2,1)} %get-tuple-element.74.dq_ref, ...), custom_call_target="tpu_custom_call" | custom-call | tf_op jit(solution)/shard_map/proj_bwd/pallas_call | solution.py:553
  362.1 1.9 convert_element_type.56
  365.3 2.0 pad_maximum_fusion.1
  367.4 4.6 convert.10
  371.9 1.1 convert_element_type.60
  373.1 1.7 slice-done.1
  375.5 2.4 constant_dynamic-update-slice_fusion.19
  378.3 1.2 constant_dynamic-update-slice_fusion.18
  379.4 1.1 constant_dynamic-update-slice_fusion.17
  380.6 1.1 constant_dynamic-update-slice_fusion.16
  381.7 1.1 constant_dynamic-update-slice_fusion.15
  382.8 2.6 constant_dynamic-update-slice_fusion.14
  386.2 40.0 %all-reduce.4 = (f32[8,768]{1,0:T(8,128)S(1)}, f32[1,3072]{1,0:T(1,128)S(1)}, f32[12,256]{1,0:T(8,128)S(1)}) all-reduce(f32[8,768]{1,0:T(8,128)S(1)} %pad_maximum_fusion.3, f32[1,3072]{1,0:T(1,128)S(1)} %copy-done.6, f32[12,256]{1,0:T(8,128)S(1)} %copy-done.5), channel_id=1, replica_groups=mesh['dp'=8,'fsdp'=4] {'dp','fsdp'}, use_global_device_ids=true, to_apply=%region_2.3 | all-reduce | flops 12288 | bytes 98304 | tf_op jit(solution)/shard_map/psum | solution.py:602
  428.0 41.3 %reduce-scatter.3.cloned.1.call-done = bf16[1,72,768]{2,1,0:T(8,128)(2,1)} async-done(((bf16[32,72,768]{2,1,0:T(8,128)(2,1)}), bf16[1,72,768]{2,1,0:T(8,128)(2,1)}) %reduce-scatter.3.cloned.1.call-update) | async-done | bytes 110608 | tf_op jit(solution)/shard_map/reduce_scatter | solution.py:600
  469.3 0.9 convert_element_type.59
  470.9 145.1 %reduce-scatter.5.cloned.1.call-done = bf16[1,216,768]{2,1,0:T(8,128)(2,1)} async-done(((bf16[32,216,768]{2,1,0:T(8,128)(2,1)}), bf16[1,216,768]{2,1,0:T(8,128)(2,1)}) %reduce-scatter.5.cloned.1.call-update) | async-done | bytes 331792 | tf_op jit(solution)/shard_map/reduce_scatter | solution.py:597
  616.0 1.0 convert_element_type.62
  (77 shorter events, 19.7 us)
Async XLA Ops:
  7.2 71.7 %all-gather.8.cloned.1.call-start = ((), (), s32[]{:S(2)}) async-start(), calls=%async_computation.5 | async-start | bytes 4055040 | tf_op jit(solution)/shard_map/all_gather | solution.py:577
  14.8 153.4 %all-gather.6.cloned.1.call-start = ((), (), s32[]{:S(2)}) async-start(), calls=%async_computation.4 | async-start | bytes 10948608 | tf_op jit(solution)/shard_map/all_gather | solution.py:579
  19.7 0.7 copy-start.3
  20.4 448.9 %reduce-scatter.3.cloned.1.call-start = ((), (), s32[]{:S(2)}) async-start(), calls=%async_computation.2 | async-start | bytes 3649536 | tf_op jit(solution)/shard_map/reduce_scatter | solution.py:600
  362.1 2.4 copy-start.2
  362.1 3.1 copy-start.1
  367.3 248.8 %reduce-scatter.5.cloned.1.call-start = ((), (), s32[]{:S(2)}) async-start(), calls=%async_computation.3 | async-start | bytes 10948608 | tf_op jit(solution)/shard_map/reduce_scatter | solution.py:597
  367.3 5.8 slice-start
  367.3 4.6 copy-start
  367.3 7.4 %slice-start.1 = ((s8[9437184]{0:T(1024)(128)(4,1)}), s8[4194304]{0:T(1024)(128)(4,1)S(1)}, s32[]{:S(2)}) async-start(s8[9437184]{0:T(1024)(128)(4,1)} %bitcast.117), calls=%async_computation.7 | async-start | bytes 8388608
  367.4 7.7 %slice-start.2 = ((s8[9437184]{0:T(1024)(128)(4,1)}), s8[1048576]{0:T(1024)(128)(4,1)S(1)}, s32[]{:S(2)}) async-start(s8[9437184]{0:T(1024)(128)(4,1)} %bitcast.117), calls=%async_computation.8 | async-start | bytes 2097152
  385.4 0.8 copy-start.4
  385.4 0.8 copy-start.5
  385.4 0.8 copy-start.6
Sparse Core Ops, SparseCore 0:
  15.0 63.8 all-gather.7
  82.3 85.8 all-gather.5
  367.4 101.8 reduce-scatter.2
  475.2 140.7 reduce-scatter.4

commit v2 on v1

--- a/solution.py
+++ b/solution.py
@@ -37,8 +37,8 @@
 
 
 def ffn_kernel(x_ref, att_ref, cot_ref, key_ref, wo_ref, wi_ref, wb_ref, vec_ref, bi_ref,
-               out_ref, do_ref, datt_ref, gwo_ref, gwi_ref, gwb_ref, gvec_ref, gbi_ref,
-               act_s, gp_s, sum_s, hid_s, low_s, *, chunk):
+               out_ref, do_ref, datt_ref, gwo_out, gwi_out, gwb_out, gvec_ref, gbi_ref,
+               act_s, gp_s, sum_s, hid_s, low_s, gwo_ref, gwi_ref, gwb_ref, sems, *, chunk):
     step = pl.program_id(0)
     inner = wi_ref.shape[1]
     chunks = inner // chunk
@@ -104,6 +104,33 @@
     live = (key_ref[...] >= 0).astype(F32)
     datt_ref[...] = (mm(do, wo_ref[...], NT) * live).astype(BF)
 
+    @pl.when(step == pl.num_programs(0) - 1)
+    def _():
+        d = gwo_ref.shape[0]
+        fit = act_s.shape[0] // 2
+        pieces = []
+        for r in range(0, d, fit):
+            pieces.append([(gwi_ref, gwi_out, r, inner, 0)])
+        for src, dst in ((gwb_ref, gwb_out), (gwo_ref, gwo_out)):
+            total = src.shape[0]
+            for r in range(0, total, fit * (inner // d)):
+                pieces.append([(src, dst, r + j * fit, d, j * d) for j in range(min(inner // d, (total - r) // fit))])
+        flying = [None, None]
+        for k, piece in enumerate(pieces):
+            half = k % 2
+            for c in flying[half] or ():
+                c.wait()
+            flying[half] = []
+            for src, dst, r, width, col in piece:
+                buf = act_s.at[pl.ds(half * fit, fit), pl.ds(col, width)]
+                buf[...] = src[r:r + fit, :].astype(BF)
+                flying[half].append(pltpu.make_async_copy(buf, dst.at[pl.ds(r, fit), :], sems.at[half, len(flying[half])]))
+            for c in flying[half]:
+                c.start()
+        for cs in flying:
+            for c in cs or ():
+                c.wait()
+
 
 def ffn(x, att, cot, key_col, wo, wi, wb, vec, bi, tile=512, chunk=768):
     rows, d = x.shape
@@ -115,11 +142,11 @@
         functools.partial(ffn_kernel, chunk=chunk),
         grid=(rows // tile,),
         in_specs=[row, row, row, pl.BlockSpec((tile, 1), lambda i: (i, 0)), one(d, d), one(d, inner), one(inner, d), one(8, d), one(1, inner)],
-        out_specs=[row, row, row, one(d, d), one(d, inner), one(inner, d), one(8, d), one(1, inner)],
+        out_specs=[row, row, row] + [pl.BlockSpec(memory_space=pl.ANY)] * 3 + [one(8, d), one(1, inner)],
         out_shape=[jax.ShapeDtypeStruct((rows, d), BF)] * 3 + [
-            jax.ShapeDtypeStruct((d, d), F32), jax.ShapeDtypeStruct((d, inner), F32), jax.ShapeDtypeStruct((inner, d), F32),
+            jax.ShapeDtypeStruct((d, d), BF), jax.ShapeDtypeStruct((d, inner), BF), jax.ShapeDtypeStruct((inner, d), BF),
             jax.ShapeDtypeStruct((8, d), F32), jax.ShapeDtypeStruct((1, inner), F32)],
-        scratch_shapes=[pltpu.VMEM((tile, inner), BF), pltpu.VMEM((tile, inner), F32), pltpu.VMEM((tile, d), F32), pltpu.VMEM((tile, d), F32), pltpu.VMEM((tile, d), BF)],
+        scratch_shapes=[pltpu.VMEM((tile, inner), BF), pltpu.VMEM((tile, inner), F32), pltpu.VMEM((tile, d), F32), pltpu.VMEM((tile, d), F32), pltpu.VMEM((tile, d), BF), pltpu.VMEM((d, d), F32), pltpu.VMEM((d, inner), F32), pltpu.VMEM((inner, d), F32), pltpu.SemaphoreType.DMA((2, 4))],
         compiler_params=pltpu.CompilerParams(vmem_limit_bytes=VMEM_ALL),
         name="ffn",
     )(x, att, cot, key_col, wo, wi, wb, vec, bi)
@@ -527,7 +554,7 @@
     )(datt, *[sv[k] for k in names], keyc, keyr, kwin, lkc, cwb)
 
 
-def proj_kernel(x_ref, do_ref, dq_ref, dk_ref, dv_ref, wq_ref, wk_ref, wv_ref, gt_ref, gwq_ref, gwk_ref, gwv_ref, gb_ref):
+def proj_kernel(x_ref, do_ref, dq_ref, dk_ref, dv_ref, wq_ref, wk_ref, wv_ref, gt_ref, oq_ref, ok_ref, ov_ref, gb_ref, gwq_ref, gwk_ref, gwv_ref):
     @pl.when(pl.program_id(0) == 0)
     def _():
         for ref in (gwq_ref, gwk_ref, gwv_ref, gb_ref):
@@ -542,6 +569,11 @@
     gt = do_ref[...].astype(F32) + mm(dq_ref[...], wq_ref[...], NT)
     gt = gt + mm(dk_ref[...], wk_ref[...], NT)
     gt_ref[...] = (gt + mm(dv_ref[...], wv_ref[...], NT)).astype(BF)
+
+    @pl.when(pl.program_id(0) == pl.num_programs(0) - 1)
+    def _():
+        for out, acc in ((oq_ref, gwq_ref), (ok_ref, gwk_ref), (ov_ref, gwv_ref)):
+            out[...] = acc[...].astype(BF)
 
 
 def proj_bwd(x, do, dq, dk, dv, wq, wk, wv, tile=1024):
@@ -554,18 +586,264 @@
         proj_kernel, grid=(rows // tile,),
         in_specs=[row] * 5 + [one(d, d)] * 3,
         out_specs=[row] + [one(d, d)] * 3 + [one(8, d)],
-        out_shape=[S((rows, d), BF)] + [S((d, d), F32)] * 3 + [S((8, d), F32)],
+        out_shape=[S((rows, d), BF)] + [S((d, d), BF)] * 3 + [S((8, d), F32)],
+        scratch_shapes=[pltpu.VMEM((d, d), F32)] * 3,
         compiler_params=pltpu.CompilerParams(vmem_limit_bytes=VMEM_ALL),
         name="proj_bwd",
     )(x, do, dq, dk, dv, wq, wk, wv)
 
+MESH = pl.DeviceIdType.MESH
+
+
+class Place:
+    def __init__(self, dp, fsdp):
+        self.size = dict(z=dp // 2, y=2, x=fsdp // 2, c=2)
+        i, j = lax.axis_index("dp"), lax.axis_index("fsdp")
+        self.at = dict(z=i // 2, y=i % 2, x=j // 2, c=j % 2)
+
+    def shift(self, axis, step):
+        at = dict(self.at)
+        at[axis] = lax.rem(at[axis] + step, self.size[axis])
+        return at
+
+    def device(self, at):
+        return (at["z"] * 2 + at["y"], at["x"] * 2 + at["c"])
+
+    def index(self, at):
+        s = self.size
+        return ((at["z"] * s["y"] + at["y"]) * s["x"] + at["x"]) * s["c"] + at["c"]
+
+    def peers(self, axis):
+        return [self.shift(axis, k) for k in range(1, self.size[axis])]
+
+    def blocks(self, free, at):
+        out = [dict(at)]
+        for a in "zyxc":
+            if a in free:
+                out = [dict(o, **{a: v}) for o in out for v in range(self.size[a])]
+        return out
+
+
+def greet(place):
+    barrier = pltpu.get_barrier_semaphore()
+    count = 0
+    for a in "zyxc":
+        for at in place.peers(a):
+            pl.semaphore_signal(barrier, inc=1, device_id=place.device(at), device_id_type=MESH)
+            count += 1
+    pl.semaphore_wait(barrier, count)
+
+
+def send(src, dst, ssem, rsem, dev):
+    return pltpu.make_async_remote_copy(src_ref=src, dst_ref=dst, send_sem=ssem, recv_sem=rsem, device_id=dev, device_id_type=MESH)
+
+
+def units_of(part, d, parts):
+    out = [(0, None), (1, None), (2, None), (3, None)]
+    out += [(4, (slice(None), pl.ds(c * d, d))) for c in range(parts)]
+    return out + [(5, (pl.ds(c * part, part), slice(None))) for c in range(parts)]
+
+
+def unit_view(refs, unit, lead=None):
+    a, cut = unit
+    index = (() if lead is None else (lead,)) + (() if cut is None else cut)
+    return refs[a].at[index] if index else refs[a]
+
+
+class Gather:
+    def __init__(self, place, own, to, units, orders, ssem, rsem, lsem):
+        self.place, self.own, self.to, self.units, self.orders = place, own, to, units, orders
+        self.ssem, self.rsem, self.lsem = ssem, rsem, lsem
+        self.me = place.index(place.at)
+
+    def copies(self, u, st):
+        p, unit, order = self.place, self.units[u], self.orders[u]
+        free, axis = order[:st], order[st]
+        out = []
+        for b in p.blocks(free, p.at):
+            dst = unit_view(self.to, unit, p.index(b))
+            src = unit_view(self.own, unit) if st == 0 else dst
+            for at in p.peers(axis):
+                out.append(send(src, dst, self.ssem.at[u, st], self.rsem.at[u, st], p.device(at)))
+        return out
+
+    def all_of(self, u, st):
+        p, order = self.place, self.orders[u]
+        count = (p.size[order[st]] - 1) * len(p.blocks(order[:st], p.at))
+        ref = unit_view(self.to, self.units[u], pl.ds(0, count))
+        return send(ref, ref, self.ssem.at[u, st], self.rsem.at[u, st], p.device(p.peers(order[st])[0]))
+
+    def local(self, u):
+        return pltpu.make_async_copy(unit_view(self.own, self.units[u]), unit_view(self.to, self.units[u], self.me), self.lsem.at[u])
+
+    def start(self, us):
+        for u in us:
+            for c in self.copies(u, 0):
+                c.start()
+            self.local(u).start()
+
+    def advance(self, u, st):
+        self.all_of(u, st).wait_recv()
+        if st == 0:
+            self.local(u).wait()
+        if st < 3:
+            for c in self.copies(u, st + 1):
+                c.start()
+
+    def drain(self, us):
+        for u in us:
+            for st in range(4):
+                self.all_of(u, st).wait_send()
+
+
+def gather_kernel(q_ref, k_ref, v_ref, o_ref, i_ref, b_ref, s_ref, gq, gk, gv, go, gi, gb, gs, ssem, rsem, lsem, *, dp, fsdp):
+    place = Place(dp, fsdp)
+    greet(place)
+    part, d = q_ref.shape
+    units = units_of(part, d, i_ref.shape[1] // d) + [(6, None)]
+    n = len(units)
+    g = Gather(place, (q_ref, k_ref, v_ref, o_ref, i_ref, b_ref, s_ref), (gq, gk, gv, go, gi, gb, gs), units,
+               [("zyxc", "zxyc")[u % 2] for u in range(n)], ssem, rsem, lsem)
+    g.start(range(n))
+    for st in range(4):
+        for u in range(n):
+            g.advance(u, st)
+    g.drain(range(n))
+
+
+def gather_all(shards, small, dp, fsdp):
+    n = dp * fsdp
+    part, d = shards[0].shape
+    k = 4 + 2 * (shards[4].shape[1] // d) + 1
+    arrays = tuple(shards) + (small,)
+    D = pltpu.SemaphoreType.DMA
+    return pl.pallas_call(
+        functools.partial(gather_kernel, dp=dp, fsdp=fsdp),
+        in_specs=vm(7), out_specs=[pl.BlockSpec(memory_space=pl.ANY)] * 7,
+        out_shape=[jax.ShapeDtypeStruct((n,) + a.shape, a.dtype) for a in arrays],
+        scratch_shapes=[D((k, 4)), D((k, 4)), D((k,))],
+        compiler_params=pltpu.CompilerParams(collective_id=1, has_side_effects=True),
+        name="gather",
+    )(*arrays)
+
+
+def reduce_kernel(gq, gk, gv, go, gi, gb, sm_ref, oq, ok, ov, oo, oi, ob, os_ref, r1, s1, r2, s2, r3, s3, r4, m_s, mr, ssem, rsem, msem, mrem, *, dp, fsdp):
+    place = Place(dp, fsdp)
+    greet(place)
+    _, part, d = gq.shape
+    parts = units_of(part, d, gi.shape[2] // d)
+    units = len(parts)
+    ins, outs = (gq, gk, gv, go, gi, gb), (oq, ok, ov, oo, oi, ob)
+    here = place.at
+    size = place.size
+
+    def partial(u, at):
+        return unit_view(ins, parts[u], place.index(at))
+
+    orders = [("cxyz", "cyxz")[u % 2] for u in range(units)]
+
+    def rank(at, axes):
+        r = 0
+        for a in axes:
+            r = r * size[a] + at[a]
+        return r
+
+    def rest(u, st):
+        return [a for a in "zyxc" if a not in orders[u][:st]]
+
+    def outgoing(u, st, at):
+        axis = orders[u][st - 1]
+        base = dict(here)
+        base[axis] = at[axis]
+        return place.blocks(rest(u, st), base)
+
+    recv = (None, r1, r2, r3, r4)
+    sums = (None, s1, s2, s3)
+
+    def stage_copies(u, st):
+        axis = orders[u][st - 1]
+        out = []
+        for k in range(1, size[axis]):
+            at = place.shift(axis, k)
+            for b in outgoing(u, st, at):
+                src = partial(u, b) if st == 1 else sums[st - 1].at[u, rank(b, rest(u, st - 1))]
+                slot = rank(b, rest(u, st)) if st < 4 else k - 1
+                out.append(send(src, recv[st].at[u, slot], ssem.at[u, st - 1], rsem.at[u, st - 1], place.device(at)))
+        return out
+
+    def all_of(u, st):
+        whole = recv[st].at[u]
+        return send(whole, whole, ssem.at[u, st - 1], rsem.at[u, st - 1], place.device(place.shift(orders[u][st - 1], 1)))
+
+    def small_copies(st):
+        axis = "cxyz"[st - 1]
+        return [send(m_s.at[st - 1], mr.at[st - 1, k - 1], msem.at[st - 1, k - 1], mrem.at[st - 1, k - 1], place.device(place.shift(axis, k)))
+                for k in range(1, size[axis])]
+
+    m_s[0] = sm_ref[...]
+    for u in range(units):
+        for c in stage_copies(u, 1):
+            c.start()
+    small = small_copies(1)
+    for c in small:
+        c.start()
+    for st in range(1, 5):
+        for c in small:
+            c.wait()
+        total = m_s[st - 1]
+        for k in range(len(small)):
+            total = total + mr[st - 1, k]
+        if st < 4:
+            m_s[st] = total
+            small = small_copies(st + 1)
+            for c in small:
+                c.start()
+        else:
+            os_ref[...] = total
+        for u in range(units):
+            all_of(u, st).wait_recv()
+            if st < 4:
+                for b in place.blocks(rest(u, st), here):
+                    mine = partial(u, b)[...] if st == 1 else sums[st - 1][u, rank(b, rest(u, st - 1))]
+                    slot = rank(b, rest(u, st))
+                    sums[st][u, slot] = (mine.astype(F32) + recv[st][u, slot].astype(F32)).astype(BF)
+                for c in stage_copies(u, st + 1):
+                    c.start()
+            else:
+                t = s3[u, here["z"]].astype(F32)
+                for k in range(size["z"] - 1):
+                    t = t + r4[u, k].astype(F32)
+                unit_view(outs, parts[u])[...] = t
+    for u in range(units):
+        for st in range(1, 5):
+            all_of(u, st).wait_send()
+
+
+def reduce_all(grads, sm, dp, fsdp):
+    n, part, d = grads[0].shape
+    k = 4 + 2 * (grads[4].shape[2] // d)
+    S = jax.ShapeDtypeStruct
+    V = pltpu.VMEM
+    D = pltpu.SemaphoreType.DMA
+    z, x = dp // 2, fsdp // 2
+    blk = lambda m: V((k, m, part, d), BF)
+    return pl.pallas_call(
+        functools.partial(reduce_kernel, dp=dp, fsdp=fsdp),
+        in_specs=vm(7), out_specs=vm(7),
+        out_shape=[S(g.shape[1:], F32) for g in grads] + [S(sm.shape, F32)],
+        scratch_shapes=[blk(z * 2 * x), blk(z * 2 * x), blk(z * 2), blk(z * 2), blk(z), blk(z), blk(z - 1),
+                        V((4,) + sm.shape, F32), V((4, z - 1) + sm.shape, F32), D((k, 4)), D((k, 4)), D((4, z - 1)), D((4, z - 1))],
+        compiler_params=pltpu.CompilerParams(collective_id=2, has_side_effects=True, vmem_limit_bytes=VMEM_ALL),
+        name="reduce",
+    )(*grads, sm)
+
 
 AXES = ("dp", "fsdp")
 LAND = 64
 PINV_STEPS = 6
 
 
-def per_device(tokens, seg_ids, pad_mask, w_query, w_key, w_value, w_out, w_in, w_back, b_query, b_value, b_out,
+def per_device_native(tokens, seg_ids, pad_mask, w_query, w_key, w_value, w_out, w_in, w_back, b_query, b_value, b_out,
                gain_attn, shift_attn, b_in, b_back, gain_ffn, shift_ffn, conv_weight, cotangent):
     seqs, length, d = tokens.shape
     taps = conv_weight.shape[1]
@@ -592,8 +870,8 @@
     x = tokens.reshape(-1, d)
     sv = attn_fwd(x, wq, wk, wv, vec, keys, taps_f, seqs, LAND, taps, PINV_STEPS)
     out, do, datt, gwo, gwi, gwb, gvec, gbi = ffn(x, sv["att"], cotangent.reshape(-1, d), keys[0], wo, wi, wb, vec, bi, 512, 1024)
-    split_rows = lambda g: g.astype(BF).reshape(n, -1, d)
-    gi = jnp.concatenate([gwi[:, c * d:(c + 1) * d].astype(BF).reshape(n, part, d) for c in range(inner // d)], axis=1)
+    split_rows = lambda g: g.reshape(n, -1, d)
+    gi = jnp.concatenate([gwi[:, c * d:(c + 1) * d].reshape(n, part, d) for c in range(inner // d)], axis=1)
     late = lax.psum_scatter(jnp.concatenate([split_rows(gwo), gi, split_rows(gwb)], axis=1), AXES, scatter_dimension=0, tiled=True)[0].astype(F32)
     dq, dk, dv, gc = attn_bwd(datt, sv, keys, taps_b, seqs, LAND, taps)
     gt, gwq, gwk, gwv, gb = proj_bwd(x, do, dq, dk, dv, wq, wk, wv)
@@ -610,10 +888,46 @@
             vs[0], vs[1], vs[2], vs[3], vs[4], bs, vs[5], vs[6], vs[7], gc[:, :taps])
 
 
+def per_device(dp, fsdp, *args):
+    part = args[3].shape[0]
+    if part % 8 or dp % 2 or fsdp % 2:
+        return per_device_native(*args)
+    (tokens, seg_ids, pad_mask, w_query, w_key, w_value, w_out, w_in, w_back, b_query, b_value, b_out,
+     gain_attn, shift_attn, b_in, b_back, gain_ffn, shift_ffn, conv_weight, cotangent) = args
+    seqs, length, d = tokens.shape
+    taps = conv_weight.shape[1]
+    inner = w_in.shape[1]
+    n = dp * fsdp
+    share = inner // n
+    vecs = jnp.stack([b_query, b_value, b_out, gain_attn, shift_attn, b_back, gain_ffn, shift_ffn])
+    small = jnp.pad(jnp.concatenate([vecs, b_in.reshape(8, share // 8)], axis=1).astype(F32), ((0, 0), (0, 128 - part - share // 8)))
+    *weights, small = gather_all((w_query, w_key, w_value, w_out, w_in, w_back), small, dp, fsdp)
+    wq, wk, wv, wo, wi, wb = (w.reshape(-1, w.shape[2]) for w in weights)
+    vec = small[:, :, :part].transpose(1, 0, 2).reshape(8, d)
+    bi = small[:, :, part:part + share // 8].reshape(1, inner)
+    keys = make_keys(seg_ids, pad_mask, LAND, taps)
+    taps_f, taps_b = make_taps(conv_weight)
+    x = tokens.reshape(-1, d)
+    sv = attn_fwd(x, wq, wk, wv, vec, keys, taps_f, seqs, LAND, taps, PINV_STEPS)
+    out, do, datt, gwo, gwi, gwb, gvec, gbi = ffn(x, sv["att"], cotangent.reshape(-1, d), keys[0], wo, wi, wb, vec, bi, 512, 1024)
+    dq, dk, dv, gc = attn_bwd(datt, sv, keys, taps_b, seqs, LAND, taps)
+    gt, gwq, gwk, gwv, gb = proj_bwd(x, do, dq, dk, dv, wq, wk, wv)
+    heads = gc.shape[0]
+    pack = jnp.concatenate([gb[:2], gvec[2:], gbi.reshape(-1, d), gc[:, :d // heads].reshape(1, d)], axis=0)
+    pack = jnp.pad(pack, ((0, -pack.shape[0] % 8), (0, 0)))
+    *got, pack = reduce_all([g.reshape(n, -1, g.shape[1]) for g in (gwq, gwk, gwv, gwo, gwi, gwb)], pack, dp, fsdp)
+    me = lax.axis_index(AXES)
+    vs = lax.dynamic_slice(pack, (0, me * part), (8, part))
+    bs = lax.dynamic_slice(pack[8:8 + inner // d].reshape(-1), (me * share,), (share,))
+    gc = pack[8 + inner // d].reshape(heads, -1)[:, :taps]
+    return (out.reshape(tokens.shape), gt.reshape(tokens.shape), *got,
+            vs[0], vs[1], vs[2], vs[3], vs[4], bs, vs[5], vs[6], vs[7], gc)
+
+
 def solution(mesh):
     rows = P(AXES, None)
     seq = P(AXES, None, None)
     vector = P(AXES)
     in_specs = (seq, rows, rows) + (rows,) * 6 + (vector,) * 9 + (P(), seq)
     out_specs = (seq, seq) + (rows,) * 6 + (vector,) * 9 + (P(),)
-    return jax.shard_map(per_device, mesh=mesh, in_specs=in_specs, out_specs=out_specs, check_vma=False)
+    return jax.shard_map(functools.partial(per_device, mesh.shape["dp"], mesh.shape["fsdp"]), mesh=mesh, in_specs=in_specs, out_specs=out_specs, check_vma=False)

time: 634 us -> 472 us (0.74)
  waiting for transfers between devices: 270 us -> 0 us
  Pallas kernels: 232 us -> 432 us
  blocking collectives: 40 us -> 0 us
  local copies, waits for them, and re-layouts: 52 us -> 28.7 us
  other arithmetic: 17.7 us -> 3.42 us
  between operations: 14.4 us -> 1.19 us
    pallas_call x0 -> x2, Pallas kernels: none -> 199 us  [the longest x1 106 us: reduce_all(): pl.pallas_call(functools.partial(reduce_kernel, dp=dp, fsdp=fsdp), in_spe...]
    reduce_scatter x2 -> x0, waiting for transfers between devices: 186 us -> none  [the longest x1 145 us: per_device(): lax.psum_scatter(jnp.concatenate([split_rows(gwo), gi, split_rows(gwb)],...]
    all_gather x2 -> x0, waiting for transfers between devices: 83.6 us -> none  [the longest x1 50.2 us: per_device(): lax.all_gather(jnp.concatenate([w_query, w_key, w_value, small], axis=0)[...]
    psum x1 -> x0, blocking collectives: 40 us -> none  [per_device(): gvec, gbi, gc = lax.psum((gvec, gbi, gc), AXES)]
    slice x11 -> x6, local copies, waits for them, and re-layouts: 17.5 us -> 4.67 us  [the longest x1 0.99 us: per_device(): bi = small[:, :, part:part + share // 8].reshape(1, inner)]
    concatenate x3 -> x0, local copies, waits for them, and re-layouts: 9.61 us -> none  [the longest x1 6.1 us: per_device(): jnp.concatenate([b_query, b_value, b_out, gain_attn, shift_attn, b_back,...]
    unnamed x40 -> x15, local copies, waits for them, and re-layouts: 16.5 us -> 11.4 us
  transfers between devices with their start and end apart: 4 -> 0, of which waited for: 4 -> 0; matrix products, arithmetic and copies ran while one was open for 6% -> 0% of each run, Pallas kernels for 8% -> 0%
where the time goes in v2:
time: 472 us; the launch traced here: 465 us
  Pallas kernels  432 us (92%)
  local copies, waits for them, and re-layouts  28.7 us (6%)
    pallas_call x1, Pallas kernels, reduce_all(): pl.pallas_call(functools.partial(reduce_kernel, dp=dp, fsdp=fsdp), in_spe...  106 us
    pallas_call x1, Pallas kernels, ffn(): pl.pallas_call(functools.partial(ffn_kernel, chunk=chunk), grid=(rows //...  106 us
    pallas_call x1, Pallas kernels, gather_all(): pl.pallas_call(functools.partial(gather_kernel, dp=dp, fsdp=fsdp), in_spe...  92.7 us
    pallas_call x1, Pallas kernels, attn_bwd(): pl.pallas_call(functools.partial(attn_bwd_kernel, seqs=seqs, length=lengt...  54.7 us
    pallas_call x1, Pallas kernels, attn_fwd(): pl.pallas_call(functools.partial(attn_fwd_kernel, seqs=seqs, length=lengt...  48.7 us
    pallas_call x1, Pallas kernels, proj_bwd(): pl.pallas_call(proj_kernel, grid=(rows // tile,), in_specs=[row] * 5 + [o...  23.8 us
    unnamed x15, local copies, waits for them, and re-layouts  11.4 us

profile of v2, /device:TPU:0, one launch (start us, length us, event | category | flops | bytes accessed | tf_op | source)
XLA Modules:
  0.0 465.3 jit_solution(16180856227382986220)
XLA Ops:
  0.7 0.7 broadcast_select_fusion
  2.8 0.8 reshape.147.lkc_ref
  4.3 0.7 reshape.121
  5.0 0.8 stack.62
  5.8 0.7 fusion.3.s_ref
  6.5 92.7 %gather.1 = (bf16[32,24,768]{2,1,0:T(8,128)(2,1)}, bf16[32,24,768]{2,1,0:T(8,128)(2,1)}, bf16[32,24,768]{2,1,0:T(8,128)(2,1)}, bf16[32,24,768]{2,1,0:T(8,128)(2,...) custom-call(bf16[24,768]{1,0:T(8,128)(2,1)} %q_ref.1, ...), custom_call_target="tpu_custom_call" | custom-call | tf_op jit(solution)/shard_map/gather/pallas_call | solution.py:720
  99.2 0.9 slice_bitcast_fusion
  100.1 0.7 reshape.125.vec_ref
  100.9 1.4 copy.53
  102.8 1.3 pad.24.cw_ref
  104.1 48.7 %attn_fwd.1 = (bf16[2048,768]{1,0:T(8,128)(2,1)}, bf16[2048,768]{1,0:T(8,128)(2,1)}, bf16[2,1152,768]{2,1,0:T(8,128)(2,1)}, bf16[128,768]{1,0:T(8,128)(2,1)}, bf...) custom-call(bf16[2048,768]{1,0:T(8,128)(2,1)} %bitcast.79, ...), custom_call_target="tpu_custom_call" | custom-call | tf_op jit(solution)/shard_map/attn_fwd/pallas_call | solution.py:355
  152.8 1.0 slice.91
  153.8 0.7 reshape.134.bi_ref
  154.5 105.8 %ffn.1 = (bf16[2048,768]{1,0:T(8,128)(2,1)}, bf16[2048,768]{1,0:T(8,128)(2,1)}, bf16[2048,768]{1,0:T(8,128)(2,1)}, bf16[768,768]{1,0:T(8,128)(2,1)}, bf16[768,30...) custom-call(bf16[2048,768]{1,0:T(8,128)(2,1)} %bitcast.80, ...), custom_call_target="tpu_custom_call" | custom-call | tf_op jit(solution)/shard_map/ffn/pallas_call | solution.py:141
  260.4 0.8 rev.3
  261.7 54.7 %attn_bwd.1 = (bf16[2048,768]{1,0:T(8,128)(2,1)}, bf16[2048,768]{1,0:T(8,128)(2,1)}, bf16[2048,768]{1,0:T(8,128)(2,1)}, f32[12,256]{1,0:T(8,128)}) custom-call(bf16[2048,768]{1,0:T(8,128)(2,1)} %get-tuple-element.77.datt_ref, bf16[2048,768]{1,0:T(8,128)(2,1)} %get-tuple-element.78.q_ref, bf16[2048,768]{1,0:T(8,128)(2,1)} %get-tuple-element.79.k_ref, ...), custom_call_target="tpu_custom_call" | custom-call | tf_op jit(solution)/shard_map/attn_bwd/pallas_call | solution.py:546
  316.4 23.8 %proj_bwd.1 = (bf16[2048,768]{1,0:T(8,128)(2,1)}, bf16[768,768]{1,0:T(8,128)(2,1)}, bf16[768,768]{1,0:T(8,128)(2,1)}, bf16[768,768]{1,0:T(8,128)(2,1)}, f32[8,768]{1,0:T(8,128)}) custom-call(bf16[2048,768]{1,0:T(8,128)(2,1)} %bitcast.81, bf16[2048,768]{1,0:T(8,128)(2,1)} %get-tuple-element.76.do_ref, bf16[2048,768]{1,0:T(8,128)(2,1)} %get-tuple-element.95.dq_ref, ...), custom_call_target="tpu_custom_call" | custom-call | tf_op jit(solution)/shard_map/proj_bwd/pallas_call | solution.py:585
  340.2 0.7 slice.92
  340.9 0.7 slice.94
  342.2 1.4 reduce.6
  343.6 0.7 slice.93
  345.0 106.3 %reduce.7 = (f32[24,768]{1,0:T(8,128)}, f32[24,768]{1,0:T(8,128)}, f32[24,768]{1,0:T(8,128)}, f32[24,768]{1,0:T(8,128)}, f32[24,3072]{1,0:T(8,128)}, /*index=5*/f32[96,768]{1,0:T(8,128)}, f32[16,768]{1,0:T(8,128)}) custom-call(bf16[32,24,768]{2,1,0:T(8,128)(2,1)} %bitcast.98, bf16[32,24,768]{2,1,0:T(8,128)(2,1)} %bitcast.99, bf16[32,24,768]{2,1,0:T(8,128)(2,1)} %bitcast.100, ...), custom_call_target="tpu_custom_call" | custom-call | tf_op jit(solution)/shard_map/reduce/pallas_call | solution.py:830
  451.3 0.7 slice.100
  452.6 0.8 constant_dynamic-slice_fusion
  454.0 0.8 slice_reduce_fusion
  454.7 0.7 reshape_squeeze.3
  455.4 1.5 copy.67
  456.9 1.5 copy.68
  458.4 1.5 copy.69
  459.9 1.5 copy.70
  461.5 1.7 copy.71
  463.2 1.7 copy.72
  (25 shorter events, 5.7 us)
